TPU v7x, 128 devices: a whole 4x4x4 slice. The times are simulated.
128 devices in a mesh: view: 4 (over y), tile: 32 (over z, x, core).
Axes of the slice: x: 4, y: 4, z: 4, core: 2. Of those that a mesh axis runs over, the one named last changes fastest.
Arguments:
- estimate: float32 [128, 768, 512], P(None, 'tile'), may hold values from 0.5 to 2
- view_stacks: float32 [4, 128, 768, 512], P('view', 'tile'), may hold values from 0 to 4
- profile_z: float32 [4, 31], P('view'), may hold values from 0.2 to 1
- profile_y: float32 [4, 15], P('view'), may hold values from 0.2 to 1
- profile_x: float32 [4, 15], P('view'), may hold values from 0.2 to 1
- offsets: int32 [4], P('view'), may hold values from -16 to 16, as said below
- coverage: int32 [32, 4], P('tile'), may hold values from 0 to 1, as said below
Outputs:
- new_estimate: float32 [128, 768, 512], P(None, 'tile')
Inputs may be any that keep to these rules, and one draw needn't show every extreme that they name: `offsets`: some view has offset 16 and some view has offset -16. `coverage`: every tile is intersected by at least one view.
All inputs are finite; a program needn't handle non-finite values.
Results may differ from a plain program's by a relative error of at most 0.0001.
Values sent between devices are 32-bit elements; how exact they have to be, the bound alone decides.
A program may use at most 192 MiB of HBM per device.

v0:
```python
import jax
import jax.numpy as jnp
from jax import lax
from jax.sharding import PartitionSpec as P

MAXOFF = 16


def with_halo(cells, sides, width):
    for axis, dim in sides:
        count = lax.axis_size(axis)
        ends = count - 1
        head = lax.slice_in_dim(cells, 0, width, axis=dim)
        tail = lax.slice_in_dim(cells, cells.shape[dim] - width, cells.shape[dim], axis=dim)
        cells = jnp.concatenate(
            [
                lax.ppermute(tail, axis, [(i, (i + 1) % count) for i in range(ends)]),
                cells,
                lax.ppermute(head, axis, [((i + 1) % count, i) for i in range(ends)]),
            ],
            axis=dim,
        )
    return cells


def band_matrix(kernel, rows_out):
    taps_count = kernel.shape[0]
    rows_in = rows_out + taps_count - 1
    out_index = jnp.arange(rows_out, dtype=jnp.int32)
    in_index = jnp.arange(rows_in, dtype=jnp.int32)
    distance = in_index[None, :] - out_index[:, None]
    tap_index = jnp.arange(taps_count, dtype=jnp.int32)
    hits = (distance[None, :, :] == tap_index[:, None, None]).astype(jnp.float32)
    return jnp.sum(hits * kernel[:, None, None], axis=0)


def band_blur(field, kernel, along):
    highest = lax.Precision.HIGHEST
    taps_count = kernel.shape[0]
    half = (taps_count - 1) // 2
    extent = field.shape[along]
    block = min(128, extent)
    count = extent // block
    widths = [(0, 0), (0, 0), (0, 0)]
    widths[along] = (half, block - half)
    padded = jnp.pad(field, widths)
    band = band_matrix(kernel, block)
    head_band = band[:, :block]
    tail_band = band[:, block:]
    head = lax.slice_in_dim(padded, 0, count * block, axis=along)
    tail = lax.slice_in_dim(padded, block, (count + 1) * block, axis=along)
    if along == 0:
        head = head.reshape((count, block) + field.shape[1:])
        tail = tail.reshape((count, block) + field.shape[1:])[:, : taps_count - 1]
        result = jnp.einsum(
            "jbyx,ob->joyx", head, head_band, precision=highest, preferred_element_type=jnp.float32
        )
        result = result + jnp.einsum(
            "jbyx,ob->joyx", tail, tail_band, precision=highest, preferred_element_type=jnp.float32
        )
        return result.reshape(field.shape)
    head = head.reshape(field.shape[:2] + (count, block))
    tail = tail.reshape(field.shape[:2] + (count, block))[..., : taps_count - 1]
    result = jnp.einsum(
        "zyjb,ob->zyjo", head, head_band, precision=highest, preferred_element_type=jnp.float32
    )
    result = result + jnp.einsum(
        "zyjb,ob->zyjo", tail, tail_band, precision=highest, preferred_element_type=jnp.float32
    )
    return result.reshape(field.shape)


def blur_rows(field, matrix_y, weights_z, weights_x):
    highest = lax.Precision.HIGHEST
    result = band_blur(field, weights_z, 0)
    result = jnp.einsum(
        "ya,zax->zyx", matrix_y, result, precision=highest, preferred_element_type=jnp.float32
    )
    return band_blur(result, weights_x, 2)


def on_device(estimate, view_stacks, profile_z, profile_y, profile_x, offsets, coverage):
    weights_z = profile_z[0] / jnp.sum(profile_z[0])
    weights_y = profile_y[0] / jnp.sum(profile_y[0])
    weights_x = profile_x[0] / jnp.sum(profile_x[0])
    row_count = estimate.shape[1]
    x_cells = estimate.shape[2]
    half_y = (weights_y.shape[0] - 1) // 2
    padded = jnp.pad(view_stacks[0], ((0, 0), (0, 0), (MAXOFF, MAXOFF)))
    shifted = lax.dynamic_slice_in_dim(padded, MAXOFF + offsets[0], x_cells, 2)
    stacked = lax.all_to_all(shifted, "tile", split_axis=1, concat_axis=0, tiled=True)
    flipped = weights_y[::-1]
    back_z = weights_z[::-1]
    back_x = weights_x[::-1]
    estimate_ext = with_halo(estimate, (("tile", 1),), half_y)
    blurred = blur_rows(estimate_ext, band_matrix(weights_y, row_count), weights_z, weights_x)
    quotient = stacked / blurred
    quotient_ext = with_halo(quotient, (("tile", 1),), half_y)
    back_blur = blur_rows(quotient_ext, band_matrix(flipped, row_count), back_z, back_x)
    view_index = lax.axis_index("view")
    covered = lax.dynamic_index_in_dim(coverage[0], view_index, 0, keepdims=False).astype(
        jnp.float32
    )
    view_count = jnp.sum(coverage[0]).astype(jnp.float32)
    weighted = covered * back_blur
    summed = lax.psum(weighted, "view")
    return estimate * summed / view_count


def solution(mesh):
    return jax.shard_map(
        on_device,
        mesh=mesh,
        in_specs=(
            P(None, "tile", None),
            P("view", "tile", None, None),
            P("view", None),
            P("view", None),
            P("view", None),
            P("view"),
            P("tile", None),
        ),
        out_specs=P(None, "tile", None),
        check_vma=False,
    )
```

profile of v0, /device:TPU:32, one launch (start us, length us, event | category | flops | bytes accessed | tf_op | source)
XLA Modules:
  0.0 460.1 jit_solution(2243969198912554570)
XLA Ops:
  6.5 6.4 %copy.65 = f32[128,24,512]{2,0,1:T(8,128)S(1)} copy(f32[128,24,512]{2,1,0:T(8,128)} %param.7) | data formatting | bytes 12582912 | tf_op args[0]
  20.1 5.9 %collective-permute-start.1 = (f32[128,7,512]{2,0,1:T(8,128)}, f32[128,7,512]{2,0,1:T(8,128)}, u32[]{:S(2)}, u32[]{:S(2)}) collective-permute-start(f32[128,7,512]{2,0,1:T(8,128)} %get-tuple-element.18), channel_id=1, source_target_pairs={{1,0},{2,1},{3,2},{4,3},{5,4},{6,5},{7,6},{8,7},{9,8},{10,9},{11,1... | collective-permute-start | bytes 5505032 | tf_op jit(solution)/shard_map/ppermute | solution.py:19
  26.7 6.7 %copy.107 = f32[1,4,768,512]{3,1,2,0:T(4,128)} copy(f32[1,4,768,512]{3,2,1,0:T(8,128)S(1)} %copy-done.4) | data formatting | bytes 12582912 | tf_op args[1]
  33.4 8.7 %pad_dynamic-slice_fusion = f32[4,768,512]{2,0,1:T(4,128)} fusion(s32[]{:T(128)S(6)} %select_n.8, f32[4,768,512]{2,0,1:T(4,128)} %bitcast.76), kind=kLoop, calls=%fused_computation.21 | loop fusion | bytes 12582916 | tf_op jit(solution)/shard_map/dynamic_slice | solution.py:90
  42.1 6.1 %all-to-all-start = ((f32[4,768,512]{2,0,1:T(4,128)}), f32[4,768,512]{2,0,1:T(4,128)}, u32[]{:S(2)}, u32[]{:S(2)}) async-start(f32[4,768,512]{2,0,1:T(4,128)} %pad_dynamic-slice_fusion), calls=%async_computation | async-start | bytes 12582912 | tf_op jit(solution)/shard_map/all_to_all | solution.py:91
  53.6 11.0 %select_maximum_fusion.2 = f32[256,38,512]{2,0,1:T(8,128)} fusion(f32[128,7,512]{2,0,1:T(8,128)} %collective-permute-done.1, f32[128,24,512]{2,0,1:T(8,128)} %copy-done, f32[128,7,512]{2,0,1:T(8,128)S(1)} %collective-permute-done), kind=kLoop, calls=%fused_computation.4 | loop fusion | flops 39845888 | bytes 29884416 | tf_op jit(solution)/shard_map/concatenate | solution.py:15
  64.6 9.5 %slice_bitcast_fusion.1 = f32[1,128,38,512]{3,1,2,0:T(8,128)} fusion(f32[256,38,512]{2,0,1:T(8,128)} %select_maximum_fusion.2), kind=kLoop, calls=%fused_computation.14 | loop fusion | bytes 19922944 | tf_op jit(solution)/shard_map/reshape | solution.py:54
  74.1 9.8 %fusion.31 = f32[128,38,512]{2,0,1:T(8,128)S(1)} fusion(f32[1,128,38,512]{3,1,2,0:T(8,128)} %slice_bitcast_fusion.1, f32[128,158]{0,1:T(8,128)S(1)} %get-tuple-element.6), kind=kOutput, calls=%fused_computation.41 | convolution fusion | flops 896532480 | bytes 12468224 | tf_op jit(solution)/shard_map/jbyx,ob->joyx/dot_general | solution.py:58
  83.9 15.1 %fusion.13 = f32[128,38,512]{2,0,1:T(8,128)S(1)} fusion(f32[128,38,512]{2,0,1:T(8,128)S(1)} %fusion.31, f32[256,38,512]{2,0,1:T(8,128)} %select_maximum_fusion.2, f32[128,158]{0,1:T(8,128)S(1)} %get-tuple-element.6), kind=kOutput, calls=%fused_computation.30 | convolution fusion | flops 3827695616 | bytes 29949952 | tf_op jit(solution)/shard_map/jbyx,ob->joyx/dot_general | solution.py:55
  99.0 18.2 %fusion.24 = f32[128,24,512]{2,1,0:T(8,128)S(1)} fusion(f32[128,38,512]{2,0,1:T(8,128)S(1)} %fusion.13, f32[24,38]{1,0:T(8,128)S(1)} %get-tuple-element.10), kind=kOutput, calls=%fused_computation.33 | convolution fusion | flops 717225984 | bytes 16256576 | tf_op jit(solution)/shard_map/ya,zax->zyx/dot_general | solution.py:76
  117.2 6.4 %pad_slice_fusion.3 = (f32[128,24,512]{2,1,0:T(8,128)}, f32[128,24,512]{2,1,0:T(8,128)}) fusion(f32[128,24,512]{2,1,0:T(8,128)S(1)} %fusion.24), kind=kLoop, calls=%fused_computation.20 | loop fusion | bytes 18874368 | tf_op jit(solution)/shard_map/slice | solution.py:50
  123.6 6.6 %copy.83 = f32[128,24,512]{0,2,1:T(8,128)} copy(f32[128,24,512]{2,1,0:T(8,128)} %get-tuple-element.16) | data formatting | bytes 12582912 | tf_op jit(solution)/shard_map/reshape | solution.py:63
  130.2 7.6 %reshape.113 = f32[128,24,4,128]{3,2,1,0:T(4,128)} reshape(f32[128,24,512]{2,1,0:T(8,128)} %get-tuple-element.15) | data formatting | bytes 12582912 | tf_op jit(solution)/shard_map/reshape | solution.py:62
  137.7 6.5 %fusion.34 = f32[128,24,4,128]{0,3,2,1:T(8,128)S(1)} fusion(f32[128,24,4,128]{0,3,2,1:T(8,128)} %bitcast.84, f32[128,142]{0,1:T(8,128)S(1)} %get-tuple-element.8), kind=kOutput, calls=%fused_computation.47 | convolution fusion | flops 264241152 | bytes 7086080 | tf_op jit(solution)/shard_map/zyjb,ob->zyjo/dot_general | solution.py:67
  144.2 10.5 %fusion.19 = f32[128,24,4,128]{0,3,2,1:T(8,128)} fusion(f32[128,24,4,128]{0,3,2,1:T(8,128)S(1)} %fusion.34, f32[128,24,4,128]{3,2,1,0:T(4,128)S(1)} %copy-done.3, f32[128,142]{0,1:T(8,128)S(1)} %get-tuple-element.8), kind=kOutput, calls=%fused_computation.32 | convolution fusion | flops 2417491968 | bytes 18939904 | tf_op jit(solution)/shard_map/zyjb,ob->zyjo/dot_general | solution.py:64
  154.7 6.6 %copy.73 = f32[128,24,512]{2,0,1:T(8,128)} copy(f32[128,24,512]{0,2,1:T(8,128)} %bitcast.81) | data formatting | bytes 12582912 | tf_op jit(solution)/shard_map/reshape | solution.py:70
  161.3 5.0 %copy.62 = f32[4,768,512]{2,1,0:T(8,128)S(1)} copy(f32[4,768,512]{2,0,1:T(4,128)} %all-to-all-done) | data formatting | bytes 12582912 | tf_op jit(solution)/shard_map/all_to_all | solution.py:91
  179.0 5.7 %collective-permute-start.3 = (f32[128,7,512]{2,0,1:T(8,128)}, f32[128,7,512]{2,0,1:T(8,128)}, u32[]{:S(2)}, u32[]{:S(2)}) collective-permute-start(f32[128,7,512]{2,0,1:T(8,128)} %get-tuple-element.14), channel_id=1, source_target_pairs={{1,0},{2,1},{3,2},{4,3},{5,4},{6,5},{7,6},{8,7},{9,8},{10,9},{11,1... | collective-permute-start | bytes 5505032 | tf_op jit(solution)/shard_map/ppermute | solution.py:19
  185.2 18.6 %collective-permute-done.2 = f32[128,7,512]{2,0,1:T(8,128)S(1)} collective-permute-done((f32[128,7,512]{2,0,1:T(8,128)}, f32[128,7,512]{2,0,1:T(8,128)S(1)}, u32[]{:S(2)}, u32[]{:S(2)}) %collective-permute-start.2) | collective-permute-done | bytes 1835040 | tf_op jit(solution)/shard_map/ppermute | solution.py:17
  205.7 11.2 %select_maximum_fusion = f32[256,38,512]{2,0,1:T(8,128)} fusion(f32[128,7,512]{2,0,1:T(8,128)} %collective-permute-done.3, f32[128,24,512]{2,0,1:T(8,128)} %copy-done.1, f32[128,7,512]{2,0,1:T(8,128)S(1)} %collective-permute-done.2), kind=kLoop, calls=%fused_computation.2 | loop fusion | flops 39845888 | bytes 29884416 | tf_op jit(solution)/shard_map/concatenate | solution.py:15
  216.9 9.5 %slice_bitcast_fusion = f32[1,128,38,512]{3,1,2,0:T(8,128)} fusion(f32[256,38,512]{2,0,1:T(8,128)} %select_maximum_fusion), kind=kLoop, calls=%fused_computation.11 | loop fusion | bytes 19922944 | tf_op jit(solution)/shard_map/reshape | solution.py:54
  226.4 9.8 %fusion.30 = f32[128,38,512]{2,0,1:T(8,128)S(1)} fusion(f32[1,128,38,512]{3,1,2,0:T(8,128)} %slice_bitcast_fusion, f32[128,158]{0,1:T(8,128)S(1)} %get-tuple-element.5), kind=kOutput, calls=%fused_computation.39 | convolution fusion | flops 896532480 | bytes 12468224 | tf_op jit(solution)/shard_map/jbyx,ob->joyx/dot_general | solution.py:58
  236.2 15.5 %fusion.16 = f32[128,38,512]{2,0,1:T(8,128)S(1)} fusion(f32[128,38,512]{2,0,1:T(8,128)S(1)} %fusion.30, f32[256,38,512]{2,0,1:T(8,128)} %select_maximum_fusion, f32[128,158]{0,1:T(8,128)S(1)} %get-tuple-element.5), kind=kOutput, calls=%fused_computation.31 | convolution fusion | flops 3827695616 | bytes 29949952 | tf_op jit(solution)/shard_map/jbyx,ob->joyx/dot_general | solution.py:55
  251.7 18.0 %fusion.27 = f32[128,24,512]{2,1,0:T(8,128)S(1)} fusion(f32[128,38,512]{2,0,1:T(8,128)S(1)} %fusion.16, f32[24,38]{1,0:T(8,128)S(1)} %get-tuple-element.9), kind=kOutput, calls=%fused_computation.34 | convolution fusion | flops 717225984 | bytes 16256576 | tf_op jit(solution)/shard_map/ya,zax->zyx/dot_general | solution.py:76
  269.7 6.4 %pad_slice_fusion.1 = (f32[128,24,512]{2,1,0:T(8,128)}, f32[128,24,512]{2,1,0:T(8,128)}) fusion(f32[128,24,512]{2,1,0:T(8,128)S(1)} %fusion.27), kind=kLoop, calls=%fused_computation.18 | loop fusion | bytes 18874368 | tf_op jit(solution)/shard_map/slice | solution.py:50
  276.1 6.6 %copy.84 = f32[128,24,512]{0,2,1:T(8,128)} copy(f32[128,24,512]{2,1,0:T(8,128)} %get-tuple-element.12) | data formatting | bytes 12582912 | tf_op jit(solution)/shard_map/reshape | solution.py:63
  282.7 7.6 %reshape.118 = f32[128,24,4,128]{3,2,1,0:T(4,128)} reshape(f32[128,24,512]{2,1,0:T(8,128)} %get-tuple-element.11) | data formatting | bytes 12582912 | tf_op jit(solution)/shard_map/reshape | solution.py:62
  290.2 6.5 %fusion.32 = f32[128,24,4,128]{0,3,2,1:T(8,128)S(1)} fusion(f32[128,24,4,128]{0,3,2,1:T(8,128)} %bitcast.83, f32[128,142]{0,1:T(8,128)S(1)} %get-tuple-element.7), kind=kOutput, calls=%fused_computation.45 | convolution fusion | flops 264241152 | bytes 7086080 | tf_op jit(solution)/shard_map/zyjb,ob->zyjo/dot_general | solution.py:67
  296.7 11.4 %add_multiply_fusion = f32[128,24,4,128]{0,3,2,1:T(8,128)} fusion(f32[128,24,4,128]{0,3,2,1:T(8,128)S(1)} %fusion.32, f32[]{:T(128)} %bitcast, f32[128,24,4,128]{3,2,1,0:T(4,128)S(1)} %copy-done.2, f32[128,142]{0,1:T(8,128)S(1)} %get-tuple-element.7), kind=kOutput, calls=%fused_computation.29 | convolution fusion | flops 2419064832 | bytes 18939908 | tf_op jit(solution)/shard_map/zyjb,ob->zyjo/dot_general | solution.py:64
  308.1 6.7 %copy.78 = f32[128,24,512]{2,1,0:T(8,128)} copy(f32[128,24,512]{0,2,1:T(8,128)} %bitcast.80) | data formatting | bytes 12582912 | tf_op jit(solution)/shard_map/mul | solution.py:105
  316.1 127.9 %all-reduce.7.cloned.1.call-done = f32[128,24,512]{2,1,0:T(8,128)} async-done(((f32[128,24,512]{2,1,0:T(8,128)}), f32[128,24,512]{2,1,0:T(8,128)}) %all-reduce.7.cloned.1.call-update) | async-done | bytes 6291472 | tf_op jit(solution)/shard_map/psum | solution.py:106
  444.1 8.9 %multiply_divide_fusion = f32[128,24,512]{2,1,0:T(8,128)} fusion(f32[128,24,512]{2,1,0:T(8,128)} %param.7, f32[128,24,512]{2,1,0:T(8,128)} %all-reduce.7.cloned.1.call-done, f32[]{:T(128)S(6)} %convert_element_type.25), kind=kLoop, calls=%fused_computation.28 | loop fusion | flops 3145728 | bytes 18874372 | tf_op jit(solution)/shard_map/div | solution.py:107
  (52 shorter events, 28.2 us)
Async XLA Ops:
  13.0 2.7 copy-start
  15.7 11.0 %copy-start.4 = (f32[1,4,768,512]{3,2,1,0:T(8,128)S(1)}, f32[1,4,768,512]{3,2,1,0:T(8,128)}, u32[]{:S(2)}) copy-start(f32[1,4,768,512]{3,2,1,0:T(8,128)} %param.8) | copy-start | bytes 18874372
  17.9 35.7 %collective-permute-start = (f32[128,7,512]{2,0,1:T(8,128)}, f32[128,7,512]{2,0,1:T(8,128)S(1)}, u32[]{:S(2)}, u32[]{:S(2)}) collective-permute-start(f32[128,7,512]{2,0,1:T(8,128)} %get-tuple-element.17), channel_id=1, source_target_pairs={{0,1},{1,2},{2,3},{3,4},{4,5},{5,6},{6,7},{7,8},{8,9},{9,10},{10,1... | collective-permute-start | bytes 5505032 | tf_op jit(solution)/shard_map/ppermute | solution.py:17
  20.1 33.5 %collective-permute-start.1 = (f32[128,7,512]{2,0,1:T(8,128)}, f32[128,7,512]{2,0,1:T(8,128)}, u32[]{:S(2)}, u32[]{:S(2)}) collective-permute-start(f32[128,7,512]{2,0,1:T(8,128)} %get-tuple-element.18), channel_id=1, source_target_pairs={{1,0},{2,1},{3,2},{4,3},{5,4},{6,5},{7,6},{8,7},{9,8},{10,9},{11,1... | collective-permute-start | bytes 5505032 | tf_op jit(solution)/shard_map/ppermute | solution.py:19
  42.1 6.6 %copy-start.7 = (f32[1,31]{1,0:T(1,128)S(1)}, f32[1,31]{1,0:T(1,128)}, u32[]{:S(2)}) copy-start(f32[1,31]{1,0:T(1,128)} %param.9) | copy-start | bytes 376
  42.1 7.3 %copy-start.5 = (f32[1,15]{1,0:T(1,128)S(1)}, f32[1,15]{1,0:T(1,128)}, u32[]{:S(2)}) copy-start(f32[1,15]{1,0:T(1,128)} %param.10) | copy-start | bytes 184
  42.1 8.0 %copy-start.6 = (f32[1,15]{1,0:T(1,128)S(1)}, f32[1,15]{1,0:T(1,128)}, u32[]{:S(2)}) copy-start(f32[1,15]{1,0:T(1,128)} %param.11) | copy-start | bytes 184
  42.1 119.2 %all-to-all-start = ((f32[4,768,512]{2,0,1:T(4,128)}), f32[4,768,512]{2,0,1:T(4,128)}, u32[]{:S(2)}, u32[]{:S(2)}) async-start(f32[4,768,512]{2,0,1:T(4,128)} %pad_dynamic-slice_fusion), calls=%async_computation | async-start | bytes 12582912 | tf_op jit(solution)/shard_map/all_to_all | solution.py:91
  48.2 395.8 %all-reduce.7.cloned.1.call-start = ((), (), s32[]{:S(2)}) async-start(), calls=%async_computation.1 | async-start | bytes 12582912 | tf_op jit(solution)/shard_map/psum | solution.py:106
  137.7 6.5 %copy-start.3 = (f32[128,24,4,128]{3,2,1,0:T(4,128)S(1)}, f32[128,24,4,128]{3,2,1,0:T(4,128)}, u32[]{:S(2)}) copy-start(f32[128,24,4,128]{3,2,1,0:T(4,128)} %reshape.113) | copy-start | bytes 18874372
  161.3 6.0 %slice-start = ((s8[6291456]{0:T(1024)(128)(4,1)}), s8[4194304]{0:T(1024)(128)(4,1)S(1)}, s32[]{:S(2)}) async-start(s8[6291456]{0:T(1024)(128)(4,1)} %bitcast.78), calls=%async_computation.2 | async-start | bytes 8388608
  166.2 1.6 slice-start.1
  172.1 2.7 copy-start.1
  174.8 9.9 %copy-start.8 = (s32[1,4]{1,0:T(1,128)S(1)}, s32[1,4]{1,0:T(1,128)}, u32[]{:S(2)}) copy-start(s32[1,4]{1,0:T(1,128)} %param.13) | copy-start | bytes 52
  177.0 26.9 %collective-permute-start.2 = (f32[128,7,512]{2,0,1:T(8,128)}, f32[128,7,512]{2,0,1:T(8,128)S(1)}, u32[]{:S(2)}, u32[]{:S(2)}) collective-permute-start(f32[128,7,512]{2,0,1:T(8,128)} %get-tuple-element.13), channel_id=1, source_target_pairs={{0,1},{1,2},{2,3},{3,4},{4,5},{5,6},{6,7},{7,8},{8,9},{9,10},{10,1... | collective-permute-start | bytes 5505032 | tf_op jit(solution)/shard_map/ppermute | solution.py:17
  179.0 26.7 %collective-permute-start.3 = (f32[128,7,512]{2,0,1:T(8,128)}, f32[128,7,512]{2,0,1:T(8,128)}, u32[]{:S(2)}, u32[]{:S(2)}) collective-permute-start(f32[128,7,512]{2,0,1:T(8,128)} %get-tuple-element.14), channel_id=1, source_target_pairs={{1,0},{2,1},{3,2},{4,3},{5,4},{6,5},{7,6},{8,7},{9,8},{10,9},{11,1... | collective-permute-start | bytes 5505032 | tf_op jit(solution)/shard_map/ppermute | solution.py:19
  290.2 6.5 %copy-start.2 = (f32[128,24,4,128]{3,2,1,0:T(4,128)S(1)}, f32[128,24,4,128]{3,2,1,0:T(4,128)}, u32[]{:S(2)}) copy-start(f32[128,24,4,128]{3,2,1,0:T(4,128)} %reshape.118) | copy-start | bytes 18874372
Sparse Core Ops, SparseCore 0:
  315.0 129.0 all-reduce.6
where the time goes:
time: 466 us; the launch traced here: 460 us
  waiting for transfers between devices  148 us (32%)
  matrix products  121 us (26%)
  local copies, waits for them, and re-layouts  112 us (24%)
  other arithmetic  41 us (9%)
  starting transfers between devices  22.3 us (5%)
  between operations  15.2 us (3%)
    psum x1, waiting for transfers between devices, on_device(): summed = lax.psum(weighted, 'view')  128 us
    dot_general x2, matrix products, blur_rows(): jnp.einsum('ya,zax->zyx', matrix_y, result, precision=highest, preferred_...  36.2 us
    dot_general x2, matrix products, band_blur(): jnp.einsum('jbyx,ob->joyx', head, head_band, precision=highest, preferred...  30.6 us
    concatenate x2, other arithmetic, with_halo(): jnp.concatenate([lax.ppermute(tail, axis, [(i, (i + 1) % count) for i in...  22.2 us
    dot_general x2, matrix products, band_blur(): jnp.einsum('zyjb,ob->zyjo', head, head_band, precision=highest, preferred...  21.9 us
    dot_general x2, matrix products, band_blur(): jnp.einsum('jbyx,ob->joyx', tail, tail_band, precision=highest, preferred...  19.5 us
    reshape x2, local copies, waits for them, and re-layouts, band_blur(): tail = tail.reshape((count, block) + field.shape[1:])[:, :taps_count - 1]  19.1 us
    unnamed x24, local copies, waits for them, and re-layouts  19.1 us
  transfers between devices with their start and end apart: 6, of which 3 were waited for; matrix products, arithmetic and copies ran while one was open for 28% of the time, Pallas kernels for 0%

commit v1 on v0

v1 whole, which is shorter than its diff:
```python
import functools

import jax
import jax.numpy as jnp
from jax import lax
from jax.experimental import pallas as pl
from jax.experimental.pallas import tpu as pltpu
from jax.sharding import PartitionSpec as P

MESH = pl.DeviceIdType.MESH
CORES = 2
LANES = 128
F32 = jnp.float32
BF16 = jnp.bfloat16


def rl_kernel(
    dims,
    est_hbm,
    stack_hbm,
    pz_ref,
    py_ref,
    px_ref,
    off_ref,
    cov_ref,
    out_hbm,
    slab,
    reg,
    est_ext,
    zb,
    q_ext,
    part,
    r1,
    r2,
    out_buf,
    yq,
    az,
    azt,
    wx,
    wxt,
    slab_sem,
    est_load,
    own_sem,
    est_send,
    est_recv,
    a2a_send,
    a2a_recv,
    qh_send,
    qh_recv,
    s1_send,
    s1_recv,
    s2_send,
    s2_recv,
    g1_send,
    g1_recv,
    g2_send,
    g2_recv,
    out_sem,
):
    nv, nt, tx, nz, ny, nx, kz, ky, kx = dims
    planes = nz // nt
    chunks = nx // LANES
    half_y = ky // 2
    half_z = kz // 2
    half_x = kx // 2
    pad = 8
    tz = nt // (tx * CORES)
    blk = nz // nv
    hb = blk // 2

    me_v = lax.axis_index("view")
    me_t = lax.axis_index("tile")
    up = lax.rem(me_v + 1, nv)
    down = lax.rem(me_v + nv - 1, nv)
    across = lax.rem(me_v + 2, nv)
    core = lax.rem(me_t, CORES)
    at_x = lax.rem(me_t // CORES, tx)
    at_z = me_t // (CORES * tx)

    def at(v, t):
        return {"view": v, "tile": t}

    def peer(k):
        c = lax.rem(core + k, CORES)
        x = lax.rem(at_x + k // CORES, tx)
        z = lax.rem(at_z + k // (CORES * tx), tz)
        return (z * tx + x) * CORES + c

    def order(i):
        return lax.rem(i * 11, nt)

    def lanes(c):
        return pl.ds(c * LANES, LANES)

    def load_est(c):
        return pltpu.make_async_copy(
            est_hbm.at[:, :, lanes(c)], est_ext.at[c, :, pl.ds(pad, ny), :], est_load.at[c]
        )

    load_slab = pltpu.make_async_copy(stack_hbm.at[0], slab, slab_sem)
    load_slab.start()
    for c in range(chunks):
        load_est(c).start()

    barrier = pltpu.get_barrier_semaphore()

    def greet(k, carry):
        pl.semaphore_signal(barrier, inc=1, device_id=at(me_v, peer(k)), device_id_type=MESH)
        return carry

    lax.fori_loop(1, nt, greet, 0)
    for v in (up, down):
        pl.semaphore_signal(barrier, inc=1, device_id=at(v, me_t), device_id_type=MESH)
    pl.semaphore_wait(barrier, nt - 1 + 2)

    def est_copy(c, side):
        target = me_t - 1 if side == 0 else me_t + 1
        rows = pl.ds(0, pad) if side == 0 else pl.ds(ny - pad, pad)
        into = pl.ds(pad + ny, pad) if side == 0 else pl.ds(0, pad)
        return pltpu.make_async_remote_copy(
            src_ref=est_hbm.at[:, rows, lanes(c)],
            dst_ref=est_ext.at[c, :, into, :],
            send_sem=est_send.at[c, side],
            recv_sem=est_recv.at[c, side],
            device_id=at(me_v, lax.rem(target + nt, nt)),
            device_id_type=MESH,
        )

    has_left = me_t > 0
    has_right = me_t < nt - 1

    @pl.when(has_left)
    def _():
        for c in range(chunks):
            est_copy(c, 0).start()

    @pl.when(has_right)
    def _():
        for c in range(chunks):
            est_copy(c, 1).start()

    off = off_ref[0]
    turn = lax.rem(nx - off, nx)
    load_slab.wait()
    rows_block = 64
    lane = lax.broadcasted_iota(jnp.int32, (rows_block, nx), 1) + off
    inside = (lane >= 0) & (lane < nx)
    per_plane = slab.shape[1] // rows_block

    def shift(i, carry):
        p = i // per_plane
        r = pl.ds(pl.multiple_of(lax.rem(i, per_plane) * rows_block, rows_block), rows_block)
        slab[p, r, :] = jnp.where(inside, pltpu.roll(slab[p, r, :], turn, 1), 0.0)
        return carry

    lax.fori_loop(0, planes * per_plane, shift, 0)

    my_planes = pl.ds(me_t * planes, planes)

    def a2a_copy(c, t):
        return pltpu.make_async_remote_copy(
            src_ref=slab.at[:, pl.ds(pl.multiple_of(t * ny, 8), ny), lanes(c)],
            dst_ref=reg.at[c, my_planes],
            send_sem=a2a_send.at[c],
            recv_sem=a2a_recv.at[c],
            device_id=at(me_v, t),
            device_id_type=MESH,
        )

    for c in range(chunks):

        def send(i, carry, c=c):
            a2a_copy(c, peer(order(i))).start()
            return carry

        lax.fori_loop(1, nt, send, 0)

    def own_planes(c):
        mine = slab.at[:, pl.ds(pl.multiple_of(me_t * ny, 8), ny), lanes(c)]
        return pltpu.make_async_copy(mine, reg.at[c, my_planes], own_sem.at[c])

    for c in range(chunks):
        own_planes(c).start()

    def total(ref, count):
        return lax.fori_loop(1, count, lambda a, s: s + ref[0, a], ref[0, 0])

    def bands(ref, count, gap, scale):
        zero = jnp.zeros(gap.shape, F32)
        full = lax.fori_loop(0, count, lambda a, m: m + jnp.where(gap == a, ref[0, a], 0.0), zero)
        full = full / scale
        hi = full.astype(BF16)
        lo = (full - hi.astype(F32)).astype(BF16)
        return hi, lo

    scale_zy = jnp.full((nz, nz), total(pz_ref, kz), F32) * jnp.full((nz, nz), total(py_ref, ky), F32)
    row = lax.broadcasted_iota(jnp.int32, (nz, nz), 0)
    col = lax.broadcasted_iota(jnp.int32, (nz, nz), 1)
    for ref, gap in ((az, col - row + half_z), (azt, row - col + half_z)):
        hi, lo = bands(pz_ref, kz, gap, scale_zy)
        ref[...] = jnp.concatenate(
            [jnp.concatenate([hi, hi], axis=1), jnp.concatenate([lo, lo], axis=1)], axis=0
        )
    wide = (3 * LANES, LANES)
    scale_x = jnp.full(wide, total(px_ref, kx), F32)
    row = lax.broadcasted_iota(jnp.int32, wide, 0)
    col = lax.broadcasted_iota(jnp.int32, wide, 1) + LANES
    for ref, gap in ((wx, row - col + half_x), (wxt, col - row + half_x)):
        hi, lo = bands(px_ref, kx, gap, scale_x)
        ref[...] = jnp.concatenate([hi, lo], axis=1)

    def split(v):
        hi = v.astype(BF16)
        return hi, (v - hi.astype(F32)).astype(BF16)

    def z_pass(matrix, v):
        hi, lo = split(v)
        r = jnp.dot(matrix[...], jnp.concatenate([hi, lo], axis=0), preferred_element_type=F32)
        return r[:nz] + r[nz:]

    def x_pass(matrix, src, y0, count, c):
        first, last = max(c - 1, 0), min(c + 1, chunks - 1)
        v = src[pl.ds(y0, count), :, first * LANES : (last + 1) * LANES]
        v = v.reshape(count * nz, v.shape[2])
        hi, lo = split(v)
        w = matrix[(first - c + 1) * LANES : (last - c + 2) * LANES, :]
        r = jnp.dot(
            jnp.concatenate([hi, lo], axis=1),
            jnp.concatenate([w, w], axis=0),
            preferred_element_type=F32,
        )
        return r[:, :LANES] + r[:, LANES:]

    for c in range(chunks):
        load_est(c).wait()

    @pl.when(has_left)
    def _():
        for c in range(chunks):
            est_copy(c, 1).wait_recv()

    @pl.when(has_right)
    def _():
        for c in range(chunks):
            est_copy(c, 0).wait_recv()

    rows_ext = ny + 2 * pad

    def clear_edge(start):
        def body(i, carry):
            for c in range(chunks):
                est_ext[c, i, pl.ds(start, pad), :] = jnp.zeros((pad, LANES), F32)
            return carry

        lax.fori_loop(0, nz, body, 0)

    @pl.when(jnp.logical_not(has_left))
    def _():
        clear_edge(0)

    @pl.when(jnp.logical_not(has_right))
    def _():
        clear_edge(pad + ny)

    est_rows = est_ext.reshape(chunks, nz * rows_ext, LANES)
    first_row = pad - half_y

    def blur_z(i, carry):
        rows = pl.ds(i + first_row, nz, stride=rows_ext)
        zb[i] = z_pass(az, jnp.concatenate([est_rows[c, rows, :] for c in range(chunks)], axis=1))
        return carry

    lax.fori_loop(0, ny + 2 * half_y, blur_z, 0)

    zblock = min(32, nz)

    def blur_y(y, carry):
        def inner(j, carry):
            zs = pl.ds(pl.multiple_of(j * zblock, zblock), zblock)
            acc = py_ref[0, 0] * zb[y, zs, :]
            for b in range(1, ky):
                acc = acc + py_ref[0, b] * zb[y + b, zs, :]
            part[y, zs, :] = acc
            return carry

        return lax.fori_loop(0, nz // zblock, inner, carry)

    lax.fori_loop(0, ny, blur_y, 0)

    ygroup = 4

    def blur_x(i, carry):
        y0 = i * ygroup
        for c in range(chunks):
            r = x_pass(wx, part, y0, ygroup, c)
            q_ext[pl.ds(half_y + y0, ygroup), :, lanes(c)] = r.reshape(ygroup, nz, LANES)
        return carry

    lax.fori_loop(0, ny // ygroup, blur_x, 0)

    halo = jnp.zeros((half_y, nz, nx), F32)

    @pl.when(jnp.logical_not(has_left))
    def _():
        q_ext[pl.ds(0, half_y)] = halo

    @pl.when(jnp.logical_not(has_right))
    def _():
        q_ext[pl.ds(half_y + ny, half_y)] = halo

    cov = jnp.full((nz, LANES), cov_ref[0, me_v].astype(F32), F32)
    count = cov_ref[0, 0]
    for v in range(1, nv):
        count = count + cov_ref[0, v]
    count = jnp.full((ny, LANES), count.astype(F32), F32)

    for c in range(chunks):
        own_planes(c).wait()
    reg_rows = reg.reshape(chunks, nz * ny, LANES)

    def qh_copy(c, side):
        target = me_t - 1 if side == 0 else me_t + 1
        rows = pl.ds(half_y, half_y) if side == 0 else pl.ds(ny, half_y)
        into = pl.ds(half_y + ny, half_y) if side == 0 else pl.ds(0, half_y)
        return pltpu.make_async_remote_copy(
            src_ref=q_ext.at[rows, :, lanes(c)],
            dst_ref=q_ext.at[into, :, lanes(c)],
            send_sem=qh_send.at[c, side],
            recv_sem=qh_recv.at[c, side],
            device_id=at(me_v, lax.rem(target + nt, nt)),
            device_id_type=MESH,
        )

    def quotient(c):
        arrived = reg.at[c, pl.ds(0, nz - planes)]
        pltpu.make_async_copy(arrived, arrived, a2a_recv.at[c]).wait()

        def body(y, carry):
            v = reg_rows[c, pl.ds(y, nz, stride=ny), :]
            q_ext[half_y + y, :, lanes(c)] = v / q_ext[half_y + y, :, lanes(c)]
            return carry

        lax.fori_loop(0, ny, body, 0)

        @pl.when(has_left)
        def _():
            qh_copy(c, 0).start()

        @pl.when(has_right)
        def _():
            qh_copy(c, 1).start()

    def back_yz(c):
        @pl.when(has_left)
        def _():
            qh_copy(c, 1).wait_recv()

        @pl.when(has_right)
        def _():
            qh_copy(c, 0).wait_recv()

        def body(i, carry):
            for k in range(2):
                acc = py_ref[0, ky - 1] * q_ext[2 * i + k, :, lanes(c)]
                for b in range(1, ky):
                    acc = acc + py_ref[0, ky - 1 - b] * q_ext[2 * i + k + b, :, lanes(c)]
                yq[:, k * LANES : (k + 1) * LANES] = acc
            r = z_pass(azt, yq[...])
            for k in range(2):
                zb[2 * i + k, :, lanes(c)] = r[:, k * LANES : (k + 1) * LANES]
            return carry

        lax.fori_loop(0, ny // 2, body, 0)

    sums = reg

    def back_x(c):
        def body(i, carry):
            r = x_pass(wxt, zb, i * ygroup, ygroup, c).reshape(ygroup, nz, LANES)
            for k in range(ygroup):
                reg_rows[c, pl.ds(i * ygroup + k, nz, stride=ny), :] = cov * r[k]
            return carry

        lax.fori_loop(0, ny // ygroup, body, 0)

    def copy_to(src, dst, send, recv, c, d):
        return pltpu.make_async_remote_copy(
            src_ref=src,
            dst_ref=dst,
            send_sem=send.at[c, d],
            recv_sem=recv.at[c, d],
            device_id=at(up if d == 0 else down, me_t),
            device_id_type=MESH,
        )

    def s1_copy(c, d):
        start = across * blk + (0 if d == 0 else hb)
        return copy_to(sums.at[c, pl.ds(start, hb)], r1.at[d, c], s1_send, s1_recv, c, d)

    def s2_copy(c, d):
        start = (up if d == 0 else down) * blk
        return copy_to(sums.at[c, pl.ds(start, blk)], r2.at[d, c], s2_send, s2_recv, c, d)

    def g1_copy(c, d):
        mine = out_buf.at[c, pl.ds(me_v * blk, blk)]
        return copy_to(mine, mine, g1_send, g1_recv, c, d)

    def g2_copy(c, d):
        start = (down if d == 0 else up) * blk + (0 if d == 0 else hb)
        half = out_buf.at[c, pl.ds(start, hb)]
        return copy_to(half, half, g2_send, g2_recv, c, d)

    def out_copy(c):
        return pltpu.make_async_copy(out_buf.at[c], out_hbm.at[:, :, lanes(c)], out_sem.at[c])

    def stage1(c):
        for d in range(2):
            s1_copy(c, d).start()

    def stage2(c):
        for d in range(2):
            s1_copy(c, d).wait_recv()
            start = (up if d == 0 else down) * blk + (0 if d == 0 else hb)

            def body(i, carry, d=d, start=start):
                sums[c, start + i] = sums[c, start + i] + r1[d, c, i]
                return carry

            lax.fori_loop(0, hb, body, 0)
            s2_copy(c, d).start()

    def stage3(c):
        for d in range(2):
            s2_copy(c, d).wait_recv()

        def body(i, carry):
            z = me_v * blk + i
            merged = sums[c, z] + (r2[0, c, i] + r2[1, c, i])
            out_buf[c, z] = est_ext[c, z, pl.ds(pad, ny), :] * merged / count
            return carry

        lax.fori_loop(0, blk, body, 0)
        for d in range(2):
            g1_copy(c, d).start()

    def stage4(c):
        for d in range(2):
            g1_copy(c, d).wait_recv()
            g2_copy(c, d).start()

    def stage5(c):
        for d in range(2):
            g2_copy(c, d).wait_recv()
        out_copy(c).start()

    stages = (stage1, stage2, stage3, stage4, stage5)

    def tick(k):
        for n, stage in enumerate(stages):
            if 0 <= k - n < chunks:
                stage(k - n)

    for c in range(chunks):
        quotient(c)
        back_yz(c)
        if c >= 1:
            back_x(c - 1)
            tick(c - 1)
    back_x(chunks - 1)
    for k in range(chunks - 1, chunks + len(stages) - 1):
        tick(k)

    for c in range(chunks):
        sent = reg.at[c, pl.ds(0, nz - planes)]
        pltpu.make_async_copy(sent, sent, a2a_send.at[c]).wait()
        for d in range(2):
            s1_copy(c, d).wait_send()
            s2_copy(c, d).wait_send()
            g1_copy(c, d).wait_send()
            g2_copy(c, d).wait_send()
        out_copy(c).wait()

    @pl.when(has_left)
    def _():
        for c in range(chunks):
            est_copy(c, 0).wait_send()
            qh_copy(c, 0).wait_send()

    @pl.when(has_right)
    def _():
        for c in range(chunks):
            est_copy(c, 1).wait_send()
            qh_copy(c, 1).wait_send()


def solution(mesh):
    nv, nt = mesh.shape["view"], mesh.shape["tile"]

    def on_device(estimate, view_stacks, profile_z, profile_y, profile_x, offsets, coverage):
        nz, ny, nx = estimate.shape
        kz, ky, kx = profile_z.shape[1], profile_y.shape[1], profile_x.shape[1]
        planes = view_stacks.shape[1]
        tx = 4 if nt == 32 else 2
        chunks = nx // LANES
        pad = 8
        half_y = ky // 2
        blk = nz // nv
        hb = blk // 2
        dims = (nv, nt, tx, nz, ny, nx, kz, ky, kx)
        any_spec = pl.BlockSpec(memory_space=pl.ANY)
        smem_spec = pl.BlockSpec(memory_space=pltpu.SMEM)
        dma = pltpu.SemaphoreType.DMA
        return pl.pallas_call(
            functools.partial(rl_kernel, dims),
            out_shape=jax.ShapeDtypeStruct(estimate.shape, F32),
            in_specs=[any_spec, any_spec] + [smem_spec] * 5,
            out_specs=any_spec,
            scratch_shapes=[
                pltpu.VMEM(view_stacks.shape[1:], F32),
                pltpu.VMEM((chunks, nz, ny, LANES), F32),
                pltpu.VMEM((chunks, nz, ny + 2 * pad, LANES), F32),
                pltpu.VMEM((ny + 2 * half_y, nz, nx), F32),
                pltpu.VMEM((ny + 2 * half_y, nz, nx), F32),
                pltpu.VMEM((ny, nz, nx), F32),
                pltpu.VMEM((2, chunks, hb, ny, LANES), F32),
                pltpu.VMEM((2, chunks, blk, ny, LANES), F32),
                pltpu.VMEM((chunks, nz, ny, LANES), F32),
                pltpu.VMEM((nz, 2 * LANES), F32),
                pltpu.VMEM((2 * nz, 2 * nz), BF16),
                pltpu.VMEM((2 * nz, 2 * nz), BF16),
                pltpu.VMEM((3 * LANES, 2 * LANES), BF16),
                pltpu.VMEM((3 * LANES, 2 * LANES), BF16),
                dma,
                dma((chunks,)),
                dma((chunks,)),
                dma((chunks, 2)),
                dma((chunks, 2)),
                dma((chunks,)),
                dma((chunks,)),
            ]
            + [dma((chunks, 2))] * 10
            + [dma((chunks,))],
            compiler_params=pltpu.CompilerParams(
                collective_id=0, has_side_effects=True, vmem_limit_bytes=67_000_000
            ),
        )(estimate, view_stacks, profile_z, profile_y, profile_x, offsets, coverage)

    return jax.shard_map(
        on_device,
        mesh=mesh,
        in_specs=(
            P(None, "tile", None),
            P("view", "tile", None, None),
            P("view", None),
            P("view", None),
            P("view", None),
            P("view"),
            P("tile", None),
        ),
        out_specs=P(None, "tile", None),
        check_vma=False,
    )
```

time: 466 us -> 249 us (0.53); the launches traced: 460 us -> 249 us
  Pallas kernels: 0 us -> 242 us
  waiting for transfers between devices: 148 us -> 0 us
  matrix products: 121 us -> 0 us
  local copies, waits for them, and re-layouts: 112 us -> 6.2 us
  other arithmetic: 41 us -> 0 us
  starting transfers between devices: 22.3 us -> 0 us
  between operations: 15.2 us -> 0.66 us
    pallas_call x0 -> x1, Pallas kernels: none -> 242 us  [on_device(): pl.pallas_call(functools.partial(rl_kernel, dims), out_shape=jax.ShapeDty...]
    psum x1 -> x0, waiting for transfers between devices: 128 us -> none  [on_device(): summed = lax.psum(weighted, 'view')]
    dot_general x10 -> x0, matrix products: 121 us -> none  [the longest x2 36.2 us: blur_rows(): jnp.einsum('ya,zax->zyx', matrix_y, result, precision=highest, preferred_...]
    reshape x7 -> x0, local copies, waits for them, and re-layouts: 53.9 us -> none  [the longest x2 19.1 us: band_blur(): tail = tail.reshape((count, block) + field.shape[1:])[:, :taps_count - 1]]
    concatenate x2 -> x0, other arithmetic: 22.2 us -> none  [with_halo(): jnp.concatenate([lax.ppermute(tail, axis, [(i, (i + 1) % count) for i in...]
    ppermute x4 -> x0, waiting for transfers between devices: 20.4 us -> none  [the longest x2 18.6 us: with_halo(): lax.ppermute(tail, axis, [(i, (i + 1) % count) for i in range(ends)])]
    slice x4 -> x0, local copies, waits for them, and re-layouts: 17.2 us -> none  [the longest x2 12.8 us: band_blur(): head = lax.slice_in_dim(padded, 0, count * block, axis=along)]
    ppermute x4 -> x0, starting transfers between devices: 15.8 us -> none  [the longest x2 11.6 us: with_halo(): lax.ppermute(head, axis, [((i + 1) % count, i) for i in range(ends)])]
  transfers between devices with their start and end apart: 6 -> 0, of which waited for: 3 -> 0; matrix products, arithmetic and copies ran while one was open for 28% -> 0% of each run, Pallas kernels for 0% -> 0%
where the time goes in v1:
time: 249 us
  Pallas kernels  242 us (97%)
  local copies, waits for them, and re-layouts  6.2 us (2%)
    pallas_call x1, Pallas kernels, on_device(): pl.pallas_call(functools.partial(rl_kernel, dims), out_shape=jax.ShapeDty...  242 us
    unnamed x1, local copies, waits for them, and re-layouts  6.2 us

profile of v1, /device:TPU:32, one launch (start us, length us, event | category | flops | bytes accessed | tf_op | source)
XLA Modules:
  0.0 248.7 jit_solution(2480042370995287411)
XLA Ops:
  0.7 241.8 %shard_map.73 = f32[128,24,512]{2,1,0:T(8,128)} custom-call(f32[128,24,512]{2,1,0:T(8,128)} %est_hbm.1, f32[1,4,768,512]{3,2,1,0:T(8,128)} %stack_hbm.1, f32[1,31]{1,0:T(1,128)} %pz_ref.1, f32[1,15]{1,0:T(1,128)} %py_ref.1, f32[1,15]{1,0:T(1,128)} %px_ref.1, s32[1]{0:T(128)S(6)} %copy.9.off_ref, s32[1,4]{1,0:T(1,128)} %cov_ref.1), custom_call_target="tpu_custom_call" | custom-call | tf_op jit(solution)/shard_map/pallas_call | solution.py:513
  242.5 6.2 %copy.10 = f32[128,24,512]{2,1,0:T(8,128)} copy(f32[128,24,512]{2,1,0:T(8,128)} %shard_map.73) | data formatting | bytes 12582912

commit v2 on v1

--- a/solution.py
+++ b/solution.py
@@ -10,6 +10,7 @@
 MESH = pl.DeviceIdType.MESH
 CORES = 2
 LANES = 128
+UNITS = 2
 F32 = jnp.float32
 BF16 = jnp.bfloat16
 
@@ -66,7 +67,9 @@
     pad = 8
     tz = nt // (tx * CORES)
     blk = nz // nv
-    hb = blk // 2
+    units = UNITS
+    sub = blk // units
+    half = sub // 2
 
     me_v = lax.axis_index("view")
     me_t = lax.axis_index("tile")
@@ -80,14 +83,26 @@
     def at(v, t):
         return {"view": v, "tile": t}
 
+    def tile_at(dz, dx, dc):
+        c = lax.rem(core + dc, CORES)
+        x = lax.rem(at_x + dx, tx)
+        z = lax.rem(at_z + dz, tz)
+        return (z * tx + x) * CORES + c
+
     def peer(k):
-        c = lax.rem(core + k, CORES)
-        x = lax.rem(at_x + k // CORES, tx)
-        z = lax.rem(at_z + k // (CORES * tx), tz)
-        return (z * tx + x) * CORES + c
-
-    def order(i):
-        return lax.rem(i * 11, nt)
+        return tile_at(k // (CORES * tx), lax.rem(k // CORES, tx), lax.rem(k, CORES))
+
+    toward = jnp.where(core == 0, tx - 1, 1)
+    away = tx - toward
+    half_ring = tx // 2
+
+    def free_peer(i):
+        dx = away * lax.rem(i // CORES, 2)
+        return tile_at(i // (2 * CORES), dx, lax.rem(i, CORES))
+
+    def shared_peer(i):
+        dx = jnp.where(lax.rem(i // CORES, 2) == 0, toward, half_ring)
+        return tile_at(i // (2 * CORES), dx, lax.rem(i, CORES))
 
     def lanes(c):
         return pl.ds(c * LANES, LANES)
@@ -167,13 +182,23 @@
             device_id_type=MESH,
         )
 
-    for c in range(chunks):
-
-        def send(i, carry, c=c):
-            a2a_copy(c, peer(order(i))).start()
+    def send_free(c):
+        def send(i, carry):
+            a2a_copy(c, free_peer(i)).start()
             return carry
 
-        lax.fori_loop(1, nt, send, 0)
+        lax.fori_loop(1, nt // 2, send, 0)
+
+    def send_shared(c):
+        def send(i, carry):
+            a2a_copy(c, shared_peer(i)).start()
+            return carry
+
+        lax.fori_loop(0, nt // 2, send, 0)
+
+    for c in range(2):
+        send_shared(c)
+        send_free(c)
 
     def own_planes(c):
         mine = slab.at[:, pl.ds(pl.multiple_of(me_t * ny, 8), ny), lanes(c)]
@@ -383,101 +408,127 @@
 
         lax.fori_loop(0, ny // ygroup, body, 0)
 
-    def copy_to(src, dst, send, recv, c, d):
+    def copy_to(src, dst, send, recv, c, u, d):
         return pltpu.make_async_remote_copy(
             src_ref=src,
             dst_ref=dst,
-            send_sem=send.at[c, d],
-            recv_sem=recv.at[c, d],
+            send_sem=send.at[c, u, d],
+            recv_sem=recv.at[c, u, d],
             device_id=at(up if d == 0 else down, me_t),
             device_id_type=MESH,
         )
 
-    def s1_copy(c, d):
-        start = across * blk + (0 if d == 0 else hb)
-        return copy_to(sums.at[c, pl.ds(start, hb)], r1.at[d, c], s1_send, s1_recv, c, d)
-
-    def s2_copy(c, d):
-        start = (up if d == 0 else down) * blk
-        return copy_to(sums.at[c, pl.ds(start, blk)], r2.at[d, c], s2_send, s2_recv, c, d)
-
-    def g1_copy(c, d):
-        mine = out_buf.at[c, pl.ds(me_v * blk, blk)]
-        return copy_to(mine, mine, g1_send, g1_recv, c, d)
-
-    def g2_copy(c, d):
-        start = (down if d == 0 else up) * blk + (0 if d == 0 else hb)
-        half = out_buf.at[c, pl.ds(start, hb)]
-        return copy_to(half, half, g2_send, g2_recv, c, d)
+    def s1_copy(c, u, d):
+        start = across * blk + u * sub + (0 if d == 0 else half)
+        return copy_to(sums.at[c, pl.ds(start, half)], r1.at[d, c, u], s1_send, s1_recv, c, u, d)
+
+    def s2_copy(c, u, d):
+        start = (up if d == 0 else down) * blk + u * sub
+        return copy_to(sums.at[c, pl.ds(start, sub)], r2.at[d, c, u], s2_send, s2_recv, c, u, d)
+
+    def g1_copy(c, u, d):
+        mine = out_buf.at[c, pl.ds(me_v * blk + u * sub, sub)]
+        return copy_to(mine, mine, g1_send, g1_recv, c, u, d)
+
+    def g2_copy(c, u, d):
+        start = (down if d == 0 else up) * blk + u * sub + (0 if d == 0 else half)
+        piece = out_buf.at[c, pl.ds(start, half)]
+        return copy_to(piece, piece, g2_send, g2_recv, c, u, d)
 
     def out_copy(c):
         return pltpu.make_async_copy(out_buf.at[c], out_hbm.at[:, :, lanes(c)], out_sem.at[c])
 
     def stage1(c):
-        for d in range(2):
-            s1_copy(c, d).start()
+        for u in range(units):
+            for d in range(2):
+                s1_copy(c, u, d).start()
 
     def stage2(c):
-        for d in range(2):
-            s1_copy(c, d).wait_recv()
-            start = (up if d == 0 else down) * blk + (0 if d == 0 else hb)
-
-            def body(i, carry, d=d, start=start):
-                sums[c, start + i] = sums[c, start + i] + r1[d, c, i]
+        for u in range(units):
+            for d in range(2):
+                s1_copy(c, u, d).wait_recv()
+                start = (up if d == 0 else down) * blk + u * sub + (0 if d == 0 else half)
+
+                def body(i, carry, u=u, d=d, start=start):
+                    sums[c, start + i] = sums[c, start + i] + r1[d, c, u, i]
+                    return carry
+
+                lax.fori_loop(0, half, body, 0)
+                s2_copy(c, u, d).start()
+
+    def stage3(c):
+        for u in range(units):
+            for d in range(2):
+                s2_copy(c, u, d).wait_recv()
+
+            def body(i, carry, u=u):
+                z = me_v * blk + u * sub + i
+                merged = sums[c, z] + (r2[0, c, u, i] + r2[1, c, u, i])
+                out_buf[c, z] = est_ext[c, z, pl.ds(pad, ny), :] * merged / count
                 return carry
 
-            lax.fori_loop(0, hb, body, 0)
-            s2_copy(c, d).start()
-
-    def stage3(c):
-        for d in range(2):
-            s2_copy(c, d).wait_recv()
-
-        def body(i, carry):
-            z = me_v * blk + i
-            merged = sums[c, z] + (r2[0, c, i] + r2[1, c, i])
-            out_buf[c, z] = est_ext[c, z, pl.ds(pad, ny), :] * merged / count
-            return carry
-
-        lax.fori_loop(0, blk, body, 0)
-        for d in range(2):
-            g1_copy(c, d).start()
+            lax.fori_loop(0, sub, body, 0)
+            for d in range(2):
+                g1_copy(c, u, d).start()
 
     def stage4(c):
-        for d in range(2):
-            g1_copy(c, d).wait_recv()
-            g2_copy(c, d).start()
+        for u in range(units):
+            for d in range(2):
+                g1_copy(c, u, d).wait_recv()
+                g2_copy(c, u, d).start()
 
     def stage5(c):
-        for d in range(2):
-            g2_copy(c, d).wait_recv()
+        for u in range(units):
+            for d in range(2):
+                g2_copy(c, u, d).wait_recv()
         out_copy(c).start()
 
-    stages = (stage1, stage2, stage3, stage4, stage5)
-
-    def tick(k):
-        for n, stage in enumerate(stages):
-            if 0 <= k - n < chunks:
-                stage(k - n)
-
-    for c in range(chunks):
-        quotient(c)
-        back_yz(c)
-        if c >= 1:
-            back_x(c - 1)
-            tick(c - 1)
-    back_x(chunks - 1)
-    for k in range(chunks - 1, chunks + len(stages) - 1):
-        tick(k)
+    quotient(0)
+    send_free(2)
+    quotient(1)
+    send_shared(2)
+    send_free(3)
+    back_yz(0)
+    back_yz(1)
+    back_x(0)
+    stage1(0)
+    stage2(0)
+    quotient(2)
+    send_shared(3)
+    stage3(0)
+    back_yz(2)
+    back_x(1)
+    stage1(1)
+    stage4(0)
+    stage2(1)
+    quotient(3)
+    stage3(1)
+    back_yz(3)
+    back_x(2)
+    stage1(2)
+    back_x(3)
+    stage1(3)
+    stage5(0)
+    stage4(1)
+    stage2(2)
+    stage2(3)
+    stage3(2)
+    stage5(1)
+    stage3(3)
+    stage4(2)
+    stage4(3)
+    stage5(2)
+    stage5(3)
 
     for c in range(chunks):
         sent = reg.at[c, pl.ds(0, nz - planes)]
         pltpu.make_async_copy(sent, sent, a2a_send.at[c]).wait()
-        for d in range(2):
-            s1_copy(c, d).wait_send()
-            s2_copy(c, d).wait_send()
-            g1_copy(c, d).wait_send()
-            g2_copy(c, d).wait_send()
+        for u in range(units):
+            for d in range(2):
+                s1_copy(c, u, d).wait_send()
+                s2_copy(c, u, d).wait_send()
+                g1_copy(c, u, d).wait_send()
+                g2_copy(c, u, d).wait_send()
         out_copy(c).wait()
 
     @pl.when(has_left)
@@ -505,7 +556,7 @@
         pad = 8
         half_y = ky // 2
         blk = nz // nv
-        hb = blk // 2
+        sub = blk // UNITS
         dims = (nv, nt, tx, nz, ny, nx, kz, ky, kx)
         any_spec = pl.BlockSpec(memory_space=pl.ANY)
         smem_spec = pl.BlockSpec(memory_space=pltpu.SMEM)
@@ -522,8 +573,8 @@
                 pltpu.VMEM((ny + 2 * half_y, nz, nx), F32),
                 pltpu.VMEM((ny + 2 * half_y, nz, nx), F32),
                 pltpu.VMEM((ny, nz, nx), F32),
-                pltpu.VMEM((2, chunks, hb, ny, LANES), F32),
-                pltpu.VMEM((2, chunks, blk, ny, LANES), F32),
+                pltpu.VMEM((2, chunks, UNITS, sub // 2, ny, LANES), F32),
+                pltpu.VMEM((2, chunks, UNITS, sub, ny, LANES), F32),
                 pltpu.VMEM((chunks, nz, ny, LANES), F32),
                 pltpu.VMEM((nz, 2 * LANES), F32),
                 pltpu.VMEM((2 * nz, 2 * nz), BF16),
@@ -538,7 +589,8 @@
                 dma((chunks,)),
                 dma((chunks,)),
             ]
-            + [dma((chunks, 2))] * 10
+            + [dma((chunks, 2))] * 2
+            + [dma((chunks, UNITS, 2))] * 8
             + [dma((chunks,))],
             compiler_params=pltpu.CompilerParams(
                 collective_id=0, has_side_effects=True, vmem_limit_bytes=67_000_000

time: 249 us -> 221 us (0.89)
  Pallas kernels: 242 us -> 214 us
    pallas_call x1, Pallas kernels: 242 us -> 214 us  [on_device(): pl.pallas_call(functools.partial(rl_kernel, dims), out_shape=jax.ShapeDty...]
where the time goes in v2:
time: 221 us
  Pallas kernels  214 us (97%)
  local copies, waits for them, and re-layouts  6.2 us (3%)
    pallas_call x1, Pallas kernels, on_device(): pl.pallas_call(functools.partial(rl_kernel, dims), out_shape=jax.ShapeDty...  214 us
    unnamed x1, local copies, waits for them, and re-layouts  6.2 us

profile of v2, /device:TPU:32, one launch (start us, length us, event | category | flops | bytes accessed | tf_op | source)
XLA Modules:
  0.0 220.7 jit_solution(819713987831884374)
XLA Ops:
  0.7 213.8 %shard_map.73 = f32[128,24,512]{2,1,0:T(8,128)} custom-call(f32[128,24,512]{2,1,0:T(8,128)} %est_hbm.1, f32[1,4,768,512]{3,2,1,0:T(8,128)} %stack_hbm.1, f32[1,31]{1,0:T(1,128)} %pz_ref.1, f32[1,15]{1,0:T(1,128)} %py_ref.1, f32[1,15]{1,0:T(1,128)} %px_ref.1, s32[1]{0:T(128)S(6)} %copy.9.off_ref, s32[1,4]{1,0:T(1,128)} %cov_ref.1), custom_call_target="tpu_custom_call" | custom-call | tf_op jit(solution)/shard_map/pallas_call | solution.py:564
  214.4 6.2 %copy.10 = f32[128,24,512]{2,1,0:T(8,128)} copy(f32[128,24,512]{2,1,0:T(8,128)} %shard_map.73) | data formatting | bytes 12582912

commit v3 on v2

--- a/solution.py
+++ b/solution.py
@@ -24,7 +24,7 @@
     px_ref,
     off_ref,
     cov_ref,
-    out_hbm,
+    out_buf,
     slab,
     reg,
     est_ext,
@@ -33,7 +33,6 @@
     part,
     r1,
     r2,
-    out_buf,
     yq,
     az,
     azt,
@@ -42,8 +41,12 @@
     slab_sem,
     est_load,
     own_sem,
-    est_send,
-    est_recv,
+    inner_send,
+    inner_recv,
+    outer_send,
+    outer_recv,
+    pass_send,
+    pass_recv,
     a2a_send,
     a2a_recv,
     qh_send,
@@ -56,7 +59,6 @@
     g1_recv,
     g2_send,
     g2_recv,
-    out_sem,
 ):
     nv, nt, tx, nz, ny, nx, kz, ky, kx = dims
     planes = nz // nt
@@ -107,13 +109,16 @@
     def lanes(c):
         return pl.ds(c * LANES, LANES)
 
+    def load_slab(p):
+        return pltpu.make_async_copy(stack_hbm.at[0, p], slab.at[p], slab_sem.at[p])
+
     def load_est(c):
         return pltpu.make_async_copy(
             est_hbm.at[:, :, lanes(c)], est_ext.at[c, :, pl.ds(pad, ny), :], est_load.at[c]
         )
 
-    load_slab = pltpu.make_async_copy(stack_hbm.at[0], slab, slab_sem)
-    load_slab.start()
+    for p in range(planes):
+        load_slab(p).start()
     for c in range(chunks):
         load_est(c).start()
 
@@ -128,47 +133,78 @@
         pl.semaphore_signal(barrier, inc=1, device_id=at(v, me_t), device_id_type=MESH)
     pl.semaphore_wait(barrier, nt - 1 + 2)
 
-    def est_copy(c, side):
-        target = me_t - 1 if side == 0 else me_t + 1
-        rows = pl.ds(0, pad) if side == 0 else pl.ds(ny - pad, pad)
-        into = pl.ds(pad + ny, pad) if side == 0 else pl.ds(0, pad)
-        return pltpu.make_async_remote_copy(
-            src_ref=est_hbm.at[:, rows, lanes(c)],
-            dst_ref=est_ext.at[c, :, into, :],
-            send_sem=est_send.at[c, side],
-            recv_sem=est_recv.at[c, side],
-            device_id=at(me_v, lax.rem(target + nt, nt)),
-            device_id_type=MESH,
-        )
-
     has_left = me_t > 0
     has_right = me_t < nt - 1
-
-    @pl.when(has_left)
+    has_outer = jnp.where(core == 0, me_t, nt - 1 - me_t) > 0
+
+    def aligned(row):
+        return pl.ds(pl.multiple_of(row, 8), pad)
+
+    def inner_copy(c):
+        return pltpu.make_async_remote_copy(
+            src_ref=est_hbm.at[:, aligned((1 - core) * (ny - pad)), lanes(c)],
+            dst_ref=est_ext.at[c, :, aligned(core * (ny + pad)), :],
+            send_sem=inner_send.at[c],
+            recv_sem=inner_recv.at[c],
+            device_id=at(me_v, me_t + 1 - 2 * core),
+            device_id_type=MESH,
+        )
+
+    def outer_copy(c):
+        share = pl.ds(me_v * blk, blk)
+        return pltpu.make_async_remote_copy(
+            src_ref=est_hbm.at[share, aligned(core * (ny - pad)), lanes(c)],
+            dst_ref=est_ext.at[c, share, aligned((1 - core) * (ny + pad)), :],
+            send_sem=outer_send.at[c],
+            recv_sem=outer_recv.at[c],
+            device_id=at(me_v, lax.rem(me_t + nt - 1 + 2 * core, nt)),
+            device_id_type=MESH,
+        )
+
+    outer_rows = aligned(core * (ny + pad))
+
+    def pass_copy(n, d):
+        if n == 0:
+            share = pl.ds(me_v * blk, blk)
+        else:
+            share = pl.ds((down if d == 0 else up) * blk + d * (blk // 2), blk // 2)
+        region = est_ext.at[:, share, outer_rows, :]
+        return pltpu.make_async_remote_copy(
+            src_ref=region,
+            dst_ref=region,
+            send_sem=pass_send.at[n, d],
+            recv_sem=pass_recv.at[n, d],
+            device_id=at(up if d == 0 else down, me_t),
+            device_id_type=MESH,
+        )
+
+    @pl.when(has_outer)
     def _():
         for c in range(chunks):
-            est_copy(c, 0).start()
-
-    @pl.when(has_right)
-    def _():
-        for c in range(chunks):
-            est_copy(c, 1).start()
+            outer_copy(c).start()
+
+    for c in range(chunks):
+        inner_copy(c).start()
 
     off = off_ref[0]
-    turn = lax.rem(nx - off, nx)
-    load_slab.wait()
+    turn = lax.rem(LANES - off, LANES)
     rows_block = 64
-    lane = lax.broadcasted_iota(jnp.int32, (rows_block, nx), 1) + off
-    inside = (lane >= 0) & (lane < nx)
-    per_plane = slab.shape[1] // rows_block
-
-    def shift(i, carry):
-        p = i // per_plane
-        r = pl.ds(pl.multiple_of(lax.rem(i, per_plane) * rows_block, rows_block), rows_block)
-        slab[p, r, :] = jnp.where(inside, pltpu.roll(slab[p, r, :], turn, 1), 0.0)
-        return carry
-
-    lax.fori_loop(0, planes * per_plane, shift, 0)
+    lane = lax.broadcasted_iota(jnp.int32, (rows_block, LANES), 1) + off
+    over = lane >= LANES
+    under = lane < 0
+    nothing = jnp.zeros((rows_block, LANES), F32)
+
+    for p in range(planes):
+        load_slab(p).wait()
+
+        def shift(i, carry, p=p):
+            r = pl.ds(pl.multiple_of(i * rows_block, rows_block), rows_block)
+            v = [nothing] + [pltpu.roll(slab[p, r, lanes(c)], turn, 1) for c in range(chunks)] + [nothing]
+            for c in range(chunks):
+                slab[p, r, lanes(c)] = jnp.where(over, v[c + 2], jnp.where(under, v[c], v[c + 1]))
+            return carry
+
+        lax.fori_loop(0, slab.shape[1] // rows_block, shift, 0)
 
     my_planes = pl.ds(me_t * planes, planes)
 
@@ -256,37 +292,7 @@
         )
         return r[:, :LANES] + r[:, LANES:]
 
-    for c in range(chunks):
-        load_est(c).wait()
-
-    @pl.when(has_left)
-    def _():
-        for c in range(chunks):
-            est_copy(c, 1).wait_recv()
-
-    @pl.when(has_right)
-    def _():
-        for c in range(chunks):
-            est_copy(c, 0).wait_recv()
-
     rows_ext = ny + 2 * pad
-
-    def clear_edge(start):
-        def body(i, carry):
-            for c in range(chunks):
-                est_ext[c, i, pl.ds(start, pad), :] = jnp.zeros((pad, LANES), F32)
-            return carry
-
-        lax.fori_loop(0, nz, body, 0)
-
-    @pl.when(jnp.logical_not(has_left))
-    def _():
-        clear_edge(0)
-
-    @pl.when(jnp.logical_not(has_right))
-    def _():
-        clear_edge(pad + ny)
-
     est_rows = est_ext.reshape(chunks, nz * rows_ext, LANES)
     first_row = pad - half_y
 
@@ -294,8 +300,6 @@
         rows = pl.ds(i + first_row, nz, stride=rows_ext)
         zb[i] = z_pass(az, jnp.concatenate([est_rows[c, rows, :] for c in range(chunks)], axis=1))
         return carry
-
-    lax.fori_loop(0, ny + 2 * half_y, blur_z, 0)
 
     zblock = min(32, nz)
 
@@ -310,18 +314,64 @@
 
         return lax.fori_loop(0, nz // zblock, inner, carry)
 
-    lax.fori_loop(0, ny, blur_y, 0)
-
     ygroup = 4
 
-    def blur_x(i, carry):
-        y0 = i * ygroup
+    def blur_x(cs):
+        def body(i, carry):
+            y0 = i * ygroup
+            for c in cs:
+                r = x_pass(wx, part, y0, ygroup, c)
+                q_ext[pl.ds(half_y + y0, ygroup), :, lanes(c)] = r.reshape(ygroup, nz, LANES)
+            return carry
+
+        return body
+
+    @pl.when(has_outer)
+    def _():
         for c in range(chunks):
-            r = x_pass(wx, part, y0, ygroup, c)
-            q_ext[pl.ds(half_y + y0, ygroup), :, lanes(c)] = r.reshape(ygroup, nz, LANES)
-        return carry
-
-    lax.fori_loop(0, ny // ygroup, blur_x, 0)
+            outer_copy(c).wait_recv()
+        for d in range(2):
+            pass_copy(0, d).start()
+
+    @pl.when(jnp.logical_not(has_outer))
+    def _():
+        def body(i, carry):
+            for c in range(chunks):
+                est_ext[c, i, outer_rows, :] = jnp.zeros((pad, LANES), F32)
+            return carry
+
+        lax.fori_loop(0, nz, body, 0)
+
+    for c in range(chunks):
+        load_est(c).wait()
+    lax.fori_loop(half_y, half_y + ny, blur_z, 0)
+    lax.fori_loop(pad, ny - pad, blur_y, 0)
+
+    @pl.when(has_outer)
+    def _():
+        for d in range(2):
+            pass_copy(0, d).wait_recv()
+            pass_copy(1, d).start()
+
+    lax.fori_loop(pad // ygroup, (ny - pad) // ygroup, blur_x(range(chunks)), 0)
+    for c in range(chunks):
+        inner_copy(c).wait_recv()
+
+    @pl.when(has_outer)
+    def _():
+        for d in range(2):
+            pass_copy(1, d).wait_recv()
+
+    for first, last in ((0, half_y), (half_y + ny, ny + 2 * half_y)):
+        lax.fori_loop(first, last, blur_z, 0)
+    for first, last in ((0, pad), (ny - pad, ny)):
+        lax.fori_loop(first, last, blur_y, 0)
+
+    def blur_x_rest(cs):
+        for first, last in ((0, pad), (ny - pad, ny)):
+            lax.fori_loop(first // ygroup, last // ygroup, blur_x(cs), 0)
+
+    blur_x_rest((0, 1))
 
     halo = jnp.zeros((half_y, nz, nx), F32)
 
@@ -375,15 +425,7 @@
         def _():
             qh_copy(c, 1).start()
 
-    def back_yz(c):
-        @pl.when(has_left)
-        def _():
-            qh_copy(c, 1).wait_recv()
-
-        @pl.when(has_right)
-        def _():
-            qh_copy(c, 0).wait_recv()
-
+    def back_pairs(c, first, last):
         def body(i, carry):
             for k in range(2):
                 acc = py_ref[0, ky - 1] * q_ext[2 * i + k, :, lanes(c)]
@@ -395,7 +437,22 @@
                 zb[2 * i + k, :, lanes(c)] = r[:, k * LANES : (k + 1) * LANES]
             return carry
 
-        lax.fori_loop(0, ny // 2, body, 0)
+        lax.fori_loop(first // 2, last // 2, body, 0)
+
+    def back_inner(c):
+        back_pairs(c, pad, ny - pad)
+
+    def back_outer(c):
+        @pl.when(has_left)
+        def _():
+            qh_copy(c, 1).wait_recv()
+
+        @pl.when(has_right)
+        def _():
+            qh_copy(c, 0).wait_recv()
+
+        back_pairs(c, 0, pad)
+        back_pairs(c, ny - pad, ny)
 
     sums = reg
 
@@ -427,16 +484,13 @@
         return copy_to(sums.at[c, pl.ds(start, sub)], r2.at[d, c, u], s2_send, s2_recv, c, u, d)
 
     def g1_copy(c, u, d):
-        mine = out_buf.at[c, pl.ds(me_v * blk + u * sub, sub)]
+        mine = out_buf.at[pl.ds(me_v * blk + u * sub, sub), :, lanes(c)]
         return copy_to(mine, mine, g1_send, g1_recv, c, u, d)
 
     def g2_copy(c, u, d):
         start = (down if d == 0 else up) * blk + u * sub + (0 if d == 0 else half)
-        piece = out_buf.at[c, pl.ds(start, half)]
+        piece = out_buf.at[pl.ds(start, half), :, lanes(c)]
         return copy_to(piece, piece, g2_send, g2_recv, c, u, d)
-
-    def out_copy(c):
-        return pltpu.make_async_copy(out_buf.at[c], out_hbm.at[:, :, lanes(c)], out_sem.at[c])
 
     def stage1(c):
         for u in range(units):
@@ -464,7 +518,7 @@
             def body(i, carry, u=u):
                 z = me_v * blk + u * sub + i
                 merged = sums[c, z] + (r2[0, c, u, i] + r2[1, c, u, i])
-                out_buf[c, z] = est_ext[c, z, pl.ds(pad, ny), :] * merged / count
+                out_buf[z, :, lanes(c)] = est_ext[c, z, pl.ds(pad, ny), :] * merged / count
                 return carry
 
             lax.fori_loop(0, sub, body, 0)
@@ -481,29 +535,33 @@
         for u in range(units):
             for d in range(2):
                 g2_copy(c, u, d).wait_recv()
-        out_copy(c).start()
 
     quotient(0)
     send_free(2)
     quotient(1)
     send_shared(2)
     send_free(3)
-    back_yz(0)
-    back_yz(1)
+    back_inner(0)
+    back_inner(1)
+    back_outer(0)
+    back_outer(1)
     back_x(0)
     stage1(0)
+    blur_x_rest((2, 3))
     stage2(0)
     quotient(2)
     send_shared(3)
     stage3(0)
-    back_yz(2)
+    back_inner(2)
+    back_outer(2)
     back_x(1)
     stage1(1)
     stage4(0)
     stage2(1)
     quotient(3)
     stage3(1)
-    back_yz(3)
+    back_inner(3)
+    back_outer(3)
     back_x(2)
     stage1(2)
     back_x(3)
@@ -529,18 +587,25 @@
                 s2_copy(c, u, d).wait_send()
                 g1_copy(c, u, d).wait_send()
                 g2_copy(c, u, d).wait_send()
-        out_copy(c).wait()
+
+        inner_copy(c).wait_send()
+
+    @pl.when(has_outer)
+    def _():
+        for c in range(chunks):
+            outer_copy(c).wait_send()
+        for n in range(2):
+            for d in range(2):
+                pass_copy(n, d).wait_send()
 
     @pl.when(has_left)
     def _():
         for c in range(chunks):
-            est_copy(c, 0).wait_send()
             qh_copy(c, 0).wait_send()
 
     @pl.when(has_right)
     def _():
         for c in range(chunks):
-            est_copy(c, 1).wait_send()
             qh_copy(c, 1).wait_send()
 
 
@@ -563,9 +628,9 @@
         dma = pltpu.SemaphoreType.DMA
         return pl.pallas_call(
             functools.partial(rl_kernel, dims),
-            out_shape=jax.ShapeDtypeStruct(estimate.shape, F32),
+            out_shape=pltpu.VMEM(estimate.shape, F32),
             in_specs=[any_spec, any_spec] + [smem_spec] * 5,
-            out_specs=any_spec,
+            out_specs=pl.BlockSpec(memory_space=pltpu.VMEM),
             scratch_shapes=[
                 pltpu.VMEM(view_stacks.shape[1:], F32),
                 pltpu.VMEM((chunks, nz, ny, LANES), F32),
@@ -575,25 +640,27 @@
                 pltpu.VMEM((ny, nz, nx), F32),
                 pltpu.VMEM((2, chunks, UNITS, sub // 2, ny, LANES), F32),
                 pltpu.VMEM((2, chunks, UNITS, sub, ny, LANES), F32),
-                pltpu.VMEM((chunks, nz, ny, LANES), F32),
                 pltpu.VMEM((nz, 2 * LANES), F32),
                 pltpu.VMEM((2 * nz, 2 * nz), BF16),
                 pltpu.VMEM((2 * nz, 2 * nz), BF16),
                 pltpu.VMEM((3 * LANES, 2 * LANES), BF16),
                 pltpu.VMEM((3 * LANES, 2 * LANES), BF16),
-                dma,
-                dma((chunks,)),
-                dma((chunks,)),
-                dma((chunks, 2)),
-                dma((chunks, 2)),
+                dma((planes,)),
+                dma((chunks,)),
+                dma((chunks,)),
+                dma((chunks,)),
+                dma((chunks,)),
+                dma((chunks,)),
+                dma((chunks,)),
+                dma((2, 2)),
+                dma((2, 2)),
                 dma((chunks,)),
                 dma((chunks,)),
             ]
             + [dma((chunks, 2))] * 2
-            + [dma((chunks, UNITS, 2))] * 8
-            + [dma((chunks,))],
+            + [dma((chunks, UNITS, 2))] * 8,
             compiler_params=pltpu.CompilerParams(
-                collective_id=0, has_side_effects=True, vmem_limit_bytes=67_000_000
+                collective_id=0, has_side_effects=True, vmem_limit_bytes=60_000_000
             ),
         )(estimate, view_stacks, profile_z, profile_y, profile_x, offsets, coverage)
 

time: 221 us -> 194 us (0.88)
  Pallas kernels: 214 us -> 190 us
  local copies, waits for them, and re-layouts: 6.2 us -> 2.71 us
    pallas_call x1, Pallas kernels: 214 us -> 190 us  [on_device(): pl.pallas_call(functools.partial(rl_kernel, dims), out_shape=pltpu.VMEM(e...]
    unnamed x1, local copies, waits for them, and re-layouts: 6.2 us -> 2.71 us
where the time goes in v3:
time: 194 us; the launch traced here: 193 us
  Pallas kernels  190 us (98%)
  local copies, waits for them, and re-layouts  2.71 us (1%)
    pallas_call x1, Pallas kernels, on_device(): pl.pallas_call(functools.partial(rl_kernel, dims), out_shape=pltpu.VMEM(e...  190 us

profile of v3, /device:TPU:32, one launch (start us, length us, event | category | flops | bytes accessed | tf_op | source)
XLA Modules:
  0.0 193.4 jit_solution(18013339752051575243)
XLA Ops:
  0.7 190.1 %shard_map.73 = f32[128,24,512]{2,1,0:T(8,128)S(1)} custom-call(f32[128,24,512]{2,1,0:T(8,128)} %est_hbm.1, f32[1,4,768,512]{3,2,1,0:T(8,128)} %stack_hbm.1, f32[1,31]{1,0:T(1,128)} %pz_ref.1, f32[1,15]{1,0:T(1,128)} %py_ref.1, f32[1,15]{1,0:T(1,128)} %px_ref.1, s32[1]{0:T(128)S(6)} %copy.10.off_ref, s32[1,4]{1,0:T(1,128)} %cov_ref.1), custom_call_target="tpu_custom_call" | custom-call | tf_op jit(solution)/shard_map/pallas_call | solution.py:629
  190.7 2.7 %copy.9 = f32[128,24,512]{2,1,0:T(8,128)} copy(f32[128,24,512]{2,1,0:T(8,128)S(1)} %shard_map.73) | data formatting | bytes 12582912

commit v4 on v3

--- a/solution.py
+++ b/solution.py
@@ -11,6 +11,7 @@
 CORES = 2
 LANES = 128
 UNITS = 2
+STRIP = 8
 F32 = jnp.float32
 BF16 = jnp.bfloat16
 
@@ -38,6 +39,11 @@
     azt,
     wx,
     wxt,
+    wm,
+    strip,
+    strip_out,
+    r1s,
+    r2s,
     slab_sem,
     est_load,
     own_sem,
@@ -72,6 +78,9 @@
     units = UNITS
     sub = blk // units
     half = sub // 2
+    packed = LANES // STRIP
+    strip_planes = nz // packed
+    strip_blk = strip_planes // nv
 
     me_v = lax.axis_index("view")
     me_t = lax.axis_index("tile")
@@ -163,17 +172,17 @@
 
     outer_rows = aligned(core * (ny + pad))
 
-    def pass_copy(n, d):
+    def pass_copy(n, h, d):
         if n == 0:
             share = pl.ds(me_v * blk, blk)
         else:
             share = pl.ds((down if d == 0 else up) * blk + d * (blk // 2), blk // 2)
-        region = est_ext.at[:, share, outer_rows, :]
+        region = est_ext.at[pl.ds(h * (chunks // 2), chunks // 2), share, outer_rows, :]
         return pltpu.make_async_remote_copy(
             src_ref=region,
             dst_ref=region,
-            send_sem=pass_send.at[n, d],
-            recv_sem=pass_recv.at[n, d],
+            send_sem=pass_send.at[n, h, d],
+            recv_sem=pass_recv.at[n, h, d],
             device_id=at(up if d == 0 else down, me_t),
             device_id_type=MESH,
         )
@@ -232,9 +241,9 @@
 
         lax.fori_loop(0, nt // 2, send, 0)
 
-    for c in range(2):
-        send_shared(c)
-        send_free(c)
+    send_shared(0)
+    send_free(0)
+    send_free(1)
 
     def own_planes(c):
         mine = slab.at[:, pl.ds(pl.multiple_of(me_t * ny, 8), ny), lanes(c)]
@@ -262,12 +271,17 @@
         ref[...] = jnp.concatenate(
             [jnp.concatenate([hi, hi], axis=1), jnp.concatenate([lo, lo], axis=1)], axis=0
         )
-    wide = (3 * LANES, LANES)
-    scale_x = jnp.full(wide, total(px_ref, kx), F32)
-    row = lax.broadcasted_iota(jnp.int32, wide, 0)
-    col = lax.broadcasted_iota(jnp.int32, wide, 1) + LANES
-    for ref, gap in ((wx, row - col + half_x), (wxt, col - row + half_x)):
-        hi, lo = bands(px_ref, kx, gap, scale_x)
+    for ref, taps in ((wx, kx), (wxt, kx), (wm, kx)):
+        shape = (ref.shape[0], LANES)
+        row = lax.broadcasted_iota(jnp.int32, shape, 0)
+        col = lax.broadcasted_iota(jnp.int32, shape, 1)
+        if ref is wx:
+            gap = row - col - LANES + half_x
+        elif ref is wxt:
+            gap = col - row + LANES
+        else:
+            gap = lax.rem(col, STRIP) - row + LANES
+        hi, lo = bands(px_ref, taps, gap, jnp.full(shape, total(px_ref, kx), F32))
         ref[...] = jnp.concatenate([hi, lo], axis=1)
 
     def split(v):
@@ -279,8 +293,8 @@
         r = jnp.dot(matrix[...], jnp.concatenate([hi, lo], axis=0), preferred_element_type=F32)
         return r[:nz] + r[nz:]
 
-    def x_pass(matrix, src, y0, count, c):
-        first, last = max(c - 1, 0), min(c + 1, chunks - 1)
+    def x_pass(matrix, src, y0, count, c, reach):
+        first, last = max(c - 1, 0), min(c + reach, chunks - 1)
         v = src[pl.ds(y0, count), :, first * LANES : (last + 1) * LANES]
         v = v.reshape(count * nz, v.shape[2])
         hi, lo = split(v)
@@ -296,23 +310,34 @@
     est_rows = est_ext.reshape(chunks, nz * rows_ext, LANES)
     first_row = pad - half_y
 
-    def blur_z(i, carry):
-        rows = pl.ds(i + first_row, nz, stride=rows_ext)
-        zb[i] = z_pass(az, jnp.concatenate([est_rows[c, rows, :] for c in range(chunks)], axis=1))
-        return carry
-
-    zblock = min(32, nz)
-
-    def blur_y(y, carry):
-        def inner(j, carry):
-            zs = pl.ds(pl.multiple_of(j * zblock, zblock), zblock)
-            acc = py_ref[0, 0] * zb[y, zs, :]
-            for b in range(1, ky):
-                acc = acc + py_ref[0, b] * zb[y + b, zs, :]
-            part[y, zs, :] = acc
-            return carry
-
-        return lax.fori_loop(0, nz // zblock, inner, carry)
+    def blur_z(h):
+        cs = range(h * chunks // 2, (h + 1) * chunks // 2)
+        into = pl.ds(h * nx // 2, nx // 2)
+
+        def body(i, carry):
+            rows = pl.ds(i + first_row, nz, stride=rows_ext)
+            zb[i, :, into] = z_pass(az, jnp.concatenate([est_rows[c, rows, :] for c in cs], axis=1))
+            return carry
+
+        return body
+
+    zblock = min(64, nz)
+
+    def blur_y(h):
+        into = pl.ds(h * nx // 2, nx // 2)
+
+        def body(y, carry):
+            def inner(j, carry):
+                zs = pl.ds(pl.multiple_of(j * zblock, zblock), zblock)
+                acc = py_ref[0, 0] * zb[y, zs, into]
+                for b in range(1, ky):
+                    acc = acc + py_ref[0, b] * zb[y + b, zs, into]
+                part[y, zs, into] = acc
+                return carry
+
+            return lax.fori_loop(0, nz // zblock, inner, carry)
+
+        return body
 
     ygroup = 4
 
@@ -320,18 +345,26 @@
         def body(i, carry):
             y0 = i * ygroup
             for c in cs:
-                r = x_pass(wx, part, y0, ygroup, c)
+                r = x_pass(wx, part, y0, ygroup, c, 1)
                 q_ext[pl.ds(half_y + y0, ygroup), :, lanes(c)] = r.reshape(ygroup, nz, LANES)
             return carry
 
         return body
 
-    @pl.when(has_outer)
-    def _():
-        for c in range(chunks):
-            outer_copy(c).wait_recv()
-        for d in range(2):
-            pass_copy(0, d).start()
+    def pass_on(n, h):
+        @pl.when(has_outer)
+        def _():
+            if n == 0:
+                for c in range(h * chunks // 2, (h + 1) * chunks // 2):
+                    outer_copy(c).wait_recv()
+            for d in range(2):
+                if n > 0:
+                    pass_copy(n - 1, h, d).wait_recv()
+                if n < 2:
+                    pass_copy(n, h, d).start()
+
+    pass_on(0, 0)
+    pass_on(0, 1)
 
     @pl.when(jnp.logical_not(has_outer))
     def _():
@@ -344,34 +377,29 @@
 
     for c in range(chunks):
         load_est(c).wait()
-    lax.fori_loop(half_y, half_y + ny, blur_z, 0)
-    lax.fori_loop(pad, ny - pad, blur_y, 0)
-
-    @pl.when(has_outer)
-    def _():
-        for d in range(2):
-            pass_copy(0, d).wait_recv()
-            pass_copy(1, d).start()
-
+    lax.fori_loop(half_y, half_y + ny, blur_z(0), 0)
+    pass_on(1, 0)
+    lax.fori_loop(half_y, half_y + ny, blur_z(1), 0)
+    pass_on(1, 1)
+    for h in range(2):
+        lax.fori_loop(pad, ny - pad, blur_y(h), 0)
     lax.fori_loop(pad // ygroup, (ny - pad) // ygroup, blur_x(range(chunks)), 0)
-    for c in range(chunks):
-        inner_copy(c).wait_recv()
-
-    @pl.when(has_outer)
-    def _():
-        for d in range(2):
-            pass_copy(1, d).wait_recv()
-
-    for first, last in ((0, half_y), (half_y + ny, ny + 2 * half_y)):
-        lax.fori_loop(first, last, blur_z, 0)
-    for first, last in ((0, pad), (ny - pad, ny)):
-        lax.fori_loop(first, last, blur_y, 0)
+
+    def blur_edges(h):
+        for c in range(h * chunks // 2, (h + 1) * chunks // 2):
+            inner_copy(c).wait_recv()
+        pass_on(2, h)
+        for first, last in ((0, half_y), (half_y + ny, ny + 2 * half_y)):
+            lax.fori_loop(first, last, blur_z(h), 0)
+        for first, last in ((0, pad), (ny - pad, ny)):
+            lax.fori_loop(first, last, blur_y(h), 0)
 
     def blur_x_rest(cs):
         for first, last in ((0, pad), (ny - pad, ny)):
             lax.fori_loop(first // ygroup, last // ygroup, blur_x(cs), 0)
 
-    blur_x_rest((0, 1))
+    blur_edges(0)
+    blur_x_rest((0,))
 
     halo = jnp.zeros((half_y, nz, nx), F32)
 
@@ -455,10 +483,25 @@
         back_pairs(c, ny - pad, ny)
 
     sums = reg
+    strip_rows = strip.reshape(strip_planes * ny, LANES)
+    row = lax.broadcasted_iota(jnp.int32, (nz, LANES), 0)
+    col = lax.broadcasted_iota(jnp.int32, (nz, LANES), 1)
+    in_strip = lax.rem(row, packed) == col // STRIP
+
+    def back_strip():
+        def body(i, carry):
+            r = x_pass(wm, zb, i * ygroup, ygroup, chunks, 0).reshape(ygroup, nz, LANES)
+            for k in range(ygroup):
+                v = jnp.where(in_strip, cov * r[k], 0.0)
+                v = jnp.sum(v.reshape(strip_planes, packed, LANES), axis=1)
+                strip_rows[pl.ds(i * ygroup + k, strip_planes, stride=ny), :] = v
+            return carry
+
+        lax.fori_loop(0, ny // ygroup, body, 0)
 
     def back_x(c):
         def body(i, carry):
-            r = x_pass(wxt, zb, i * ygroup, ygroup, c).reshape(ygroup, nz, LANES)
+            r = x_pass(wxt, zb, i * ygroup, ygroup, c, 0).reshape(ygroup, nz, LANES)
             for k in range(ygroup):
                 reg_rows[c, pl.ds(i * ygroup + k, nz, stride=ny), :] = cov * r[k]
             return carry
@@ -475,128 +518,209 @@
             device_id_type=MESH,
         )
 
+    def shares(c):
+        return range(1) if c == chunks else range(units)
+
     def s1_copy(c, u, d):
-        start = across * blk + u * sub + (0 if d == 0 else half)
-        return copy_to(sums.at[c, pl.ds(start, half)], r1.at[d, c, u], s1_send, s1_recv, c, u, d)
+        if c == chunks:
+            src, dst = strip.at[pl.ds(across * strip_blk + d * (strip_blk // 2), strip_blk // 2)], r1s.at[d]
+        else:
+            start = across * blk + u * sub + (0 if d == 0 else half)
+            src, dst = sums.at[c, pl.ds(start, half)], r1.at[d, c, u]
+        return copy_to(src, dst, s1_send, s1_recv, c, u, d)
 
     def s2_copy(c, u, d):
-        start = (up if d == 0 else down) * blk + u * sub
-        return copy_to(sums.at[c, pl.ds(start, sub)], r2.at[d, c, u], s2_send, s2_recv, c, u, d)
+        owner = up if d == 0 else down
+        if c == chunks:
+            src, dst = strip.at[pl.ds(owner * strip_blk, strip_blk)], r2s.at[d]
+        else:
+            src, dst = sums.at[c, pl.ds(owner * blk + u * sub, sub)], r2.at[d, c, u]
+        return copy_to(src, dst, s2_send, s2_recv, c, u, d)
 
     def g1_copy(c, u, d):
-        mine = out_buf.at[pl.ds(me_v * blk + u * sub, sub), :, lanes(c)]
+        if c == chunks:
+            mine = strip_out.at[pl.ds(me_v * strip_blk, strip_blk)]
+        else:
+            mine = out_buf.at[pl.ds(me_v * blk + u * sub, sub), :, lanes(c)]
         return copy_to(mine, mine, g1_send, g1_recv, c, u, d)
 
     def g2_copy(c, u, d):
-        start = (down if d == 0 else up) * blk + u * sub + (0 if d == 0 else half)
-        piece = out_buf.at[pl.ds(start, half), :, lanes(c)]
+        owner = down if d == 0 else up
+        if c == chunks:
+            piece = strip_out.at[pl.ds(owner * strip_blk + d * (strip_blk // 2), strip_blk // 2)]
+        else:
+            start = owner * blk + u * sub + (0 if d == 0 else half)
+            piece = out_buf.at[pl.ds(start, half), :, lanes(c)]
         return copy_to(piece, piece, g2_send, g2_recv, c, u, d)
 
     def stage1(c):
-        for u in range(units):
+        for u in shares(c):
             for d in range(2):
                 s1_copy(c, u, d).start()
 
     def stage2(c):
-        for u in range(units):
+        for u in shares(c):
             for d in range(2):
                 s1_copy(c, u, d).wait_recv()
-                start = (up if d == 0 else down) * blk + u * sub + (0 if d == 0 else half)
-
-                def body(i, carry, u=u, d=d, start=start):
-                    sums[c, start + i] = sums[c, start + i] + r1[d, c, u, i]
-                    return carry
-
-                lax.fori_loop(0, half, body, 0)
+                owner = up if d == 0 else down
+                if c == chunks:
+                    at_plane = pl.ds(owner * strip_blk + d * (strip_blk // 2), strip_blk // 2)
+                    strip[at_plane] = strip[at_plane] + r1s[d]
+                else:
+                    start = owner * blk + u * sub + (0 if d == 0 else half)
+
+                    def body(i, carry, u=u, d=d, start=start):
+                        sums[c, start + i] = sums[c, start + i] + r1[d, c, u, i]
+                        return carry
+
+                    lax.fori_loop(0, half, body, 0)
                 s2_copy(c, u, d).start()
 
+    lane_row = lax.broadcasted_iota(jnp.int32, (ny, LANES), 1)
+    own_rows = pl.ds(pad, ny)
+
     def stage3(c):
-        for u in range(units):
+        for u in shares(c):
             for d in range(2):
                 s2_copy(c, u, d).wait_recv()
-
-            def body(i, carry, u=u):
-                z = me_v * blk + u * sub + i
-                merged = sums[c, z] + (r2[0, c, u, i] + r2[1, c, u, i])
-                out_buf[z, :, lanes(c)] = est_ext[c, z, pl.ds(pad, ny), :] * merged / count
-                return carry
-
-            lax.fori_loop(0, sub, body, 0)
+            if c == chunks:
+
+                def body(i, carry):
+                    z = me_v * strip_blk + i
+                    est = jnp.zeros((ny, LANES), F32)
+                    for k in range(packed):
+                        v = est_ext[chunks - 1, z * packed + k, own_rows, :]
+                        v = pltpu.roll(v, (k * STRIP + half_x) % LANES, 1)
+                        est = jnp.where(lane_row // STRIP == k, v, est)
+                    merged = strip[z] + (r2s[0, i] + r2s[1, i])
+                    strip_out[z] = est * merged / count
+                    return carry
+
+                lax.fori_loop(0, strip_blk, body, 0)
+            else:
+
+                def body(i, carry, u=u):
+                    z = me_v * blk + u * sub + i
+                    merged = sums[c, z] + (r2[0, c, u, i] + r2[1, c, u, i])
+                    est = pltpu.roll(est_ext[c, z, own_rows, :], half_x, 1)
+                    if c > 0:
+                        before = pltpu.roll(est_ext[c - 1, z, own_rows, :], half_x, 1)
+                        est = jnp.where(lane_row < half_x, before, est)
+                    out_buf[z, :, lanes(c)] = est * merged / count
+                    return carry
+
+                lax.fori_loop(0, sub, body, 0)
             for d in range(2):
                 g1_copy(c, u, d).start()
 
     def stage4(c):
-        for u in range(units):
+        for u in shares(c):
             for d in range(2):
                 g1_copy(c, u, d).wait_recv()
                 g2_copy(c, u, d).start()
 
     def stage5(c):
-        for u in range(units):
+        for u in shares(c):
             for d in range(2):
                 g2_copy(c, u, d).wait_recv()
 
+    def realign(c):
+        for u in shares(c):
+            for d in range(2):
+                g1_copy(c, u, d).wait_send()
+                g2_copy(c, u, d).wait_send()
+        here = lane_row < LANES - half_x
+
+        def body(i, carry):
+            for k in range(packed):
+                z = i * packed + k
+                v = pltpu.roll(out_buf[z, :, lanes(c)], LANES - half_x, 1)
+                if c == chunks - 1:
+                    after = pltpu.roll(strip_out[i], (LANES - half_x - k * STRIP) % LANES, 1)
+                else:
+                    after = pltpu.roll(out_buf[z, :, lanes(c + 1)], LANES - half_x, 1)
+                out_buf[z, :, lanes(c)] = jnp.where(here, v, after)
+            return carry
+
+        lax.fori_loop(0, nz // packed, body, 0)
+
     quotient(0)
+    send_shared(1)
     send_free(2)
+    back_inner(0)
+    blur_edges(1)
+    back_outer(0)
+    back_x(0)
+    stage1(0)
+    blur_x_rest((1,))
+    stage2(0)
     quotient(1)
     send_shared(2)
     send_free(3)
-    back_inner(0)
     back_inner(1)
-    back_outer(0)
+    stage3(0)
     back_outer(1)
-    back_x(0)
-    stage1(0)
+    back_x(1)
+    stage1(1)
     blur_x_rest((2, 3))
-    stage2(0)
+    stage4(0)
+    stage2(1)
     quotient(2)
     send_shared(3)
-    stage3(0)
     back_inner(2)
+    stage3(1)
     back_outer(2)
-    back_x(1)
-    stage1(1)
-    stage4(0)
-    stage2(1)
-    quotient(3)
-    stage3(1)
-    back_inner(3)
-    back_outer(3)
     back_x(2)
     stage1(2)
-    back_x(3)
-    stage1(3)
     stage5(0)
     stage4(1)
     stage2(2)
+    quotient(3)
+    back_inner(3)
+    stage3(2)
+    back_outer(3)
+    back_x(3)
+    stage1(3)
+    back_strip()
+    stage1(chunks)
+    stage5(1)
+    realign(0)
+    stage4(2)
     stage2(3)
-    stage3(2)
-    stage5(1)
+    stage2(chunks)
     stage3(3)
-    stage4(2)
+    stage3(chunks)
+    stage5(2)
+    realign(1)
     stage4(3)
-    stage5(2)
+    stage4(chunks)
     stage5(3)
+    realign(2)
+    stage5(chunks)
+    realign(3)
 
     for c in range(chunks):
         sent = reg.at[c, pl.ds(0, nz - planes)]
         pltpu.make_async_copy(sent, sent, a2a_send.at[c]).wait()
-        for u in range(units):
+
+        inner_copy(c).wait_send()
+    for c in range(chunks + 1):
+        for u in shares(c):
             for d in range(2):
                 s1_copy(c, u, d).wait_send()
                 s2_copy(c, u, d).wait_send()
-                g1_copy(c, u, d).wait_send()
-                g2_copy(c, u, d).wait_send()
-
-        inner_copy(c).wait_send()
+    for d in range(2):
+        g1_copy(chunks, 0, d).wait_send()
+        g2_copy(chunks, 0, d).wait_send()
 
     @pl.when(has_outer)
     def _():
         for c in range(chunks):
             outer_copy(c).wait_send()
         for n in range(2):
-            for d in range(2):
-                pass_copy(n, d).wait_send()
+            for h in range(2):
+                for d in range(2):
+                    pass_copy(n, h, d).wait_send()
 
     @pl.when(has_left)
     def _():
@@ -622,6 +746,7 @@
         half_y = ky // 2
         blk = nz // nv
         sub = blk // UNITS
+        strip_planes = nz * STRIP // LANES
         dims = (nv, nt, tx, nz, ny, nx, kz, ky, kx)
         any_spec = pl.BlockSpec(memory_space=pl.ANY)
         smem_spec = pl.BlockSpec(memory_space=pltpu.SMEM)
@@ -644,7 +769,12 @@
                 pltpu.VMEM((2 * nz, 2 * nz), BF16),
                 pltpu.VMEM((2 * nz, 2 * nz), BF16),
                 pltpu.VMEM((3 * LANES, 2 * LANES), BF16),
-                pltpu.VMEM((3 * LANES, 2 * LANES), BF16),
+                pltpu.VMEM((2 * LANES, 2 * LANES), BF16),
+                pltpu.VMEM((LANES, 2 * LANES), BF16),
+                pltpu.VMEM((strip_planes, ny, LANES), F32),
+                pltpu.VMEM((strip_planes, ny, LANES), F32),
+                pltpu.VMEM((2, strip_planes // nv // 2, ny, LANES), F32),
+                pltpu.VMEM((2, strip_planes // nv, ny, LANES), F32),
                 dma((planes,)),
                 dma((chunks,)),
                 dma((chunks,)),
@@ -652,13 +782,13 @@
                 dma((chunks,)),
                 dma((chunks,)),
                 dma((chunks,)),
-                dma((2, 2)),
-                dma((2, 2)),
+                dma((2, 2, 2)),
+                dma((2, 2, 2)),
                 dma((chunks,)),
                 dma((chunks,)),
             ]
             + [dma((chunks, 2))] * 2
-            + [dma((chunks, UNITS, 2))] * 8,
+            + [dma((chunks + 1, UNITS, 2))] * 8,
             compiler_params=pltpu.CompilerParams(
                 collective_id=0, has_side_effects=True, vmem_limit_bytes=60_000_000
             ),

time: 194 us -> 181 us (0.933)
  Pallas kernels: 190 us -> 178 us
    pallas_call x1, Pallas kernels: 190 us -> 178 us  [on_device(): pl.pallas_call(functools.partial(rl_kernel, dims), out_shape=pltpu.VMEM(e...]
where the time goes in v4:
time: 181 us
  Pallas kernels  178 us (98%)
  local copies, waits for them, and re-layouts  2.71 us (1%)
    pallas_call x1, Pallas kernels, on_device(): pl.pallas_call(functools.partial(rl_kernel, dims), out_shape=pltpu.VMEM(e...  178 us

profile of v4, /device:TPU:32, one launch (start us, length us, event | category | flops | bytes accessed | tf_op | source)
XLA Modules:
  0.0 181.1 jit_solution(7816089032178031704)
XLA Ops:
  0.7 177.7 %shard_map.73 = f32[128,24,512]{2,1,0:T(8,128)S(1)} custom-call(f32[128,24,512]{2,1,0:T(8,128)} %est_hbm.1, f32[1,4,768,512]{3,2,1,0:T(8,128)} %stack_hbm.1, f32[1,31]{1,0:T(1,128)} %pz_ref.1, f32[1,15]{1,0:T(1,128)} %py_ref.1, f32[1,15]{1,0:T(1,128)} %px_ref.1, s32[1]{0:T(128)S(6)} %copy.10.off_ref, s32[1,4]{1,0:T(1,128)} %cov_ref.1), custom_call_target="tpu_custom_call" | custom-call | tf_op jit(solution)/shard_map/pallas_call | solution.py:754
  178.4 2.7 %copy.9 = f32[128,24,512]{2,1,0:T(8,128)} copy(f32[128,24,512]{2,1,0:T(8,128)S(1)} %shard_map.73) | data formatting | bytes 12582912

commit v5 on v4

--- a/solution.py
+++ b/solution.py
@@ -109,11 +109,11 @@
 
     def free_peer(i):
         dx = away * lax.rem(i // CORES, 2)
-        return tile_at(i // (2 * CORES), dx, lax.rem(i, CORES))
+        return tile_at(lax.rem(i // (2 * CORES) + tz // 2, tz), dx, lax.rem(i, CORES))
 
     def shared_peer(i):
-        dx = jnp.where(lax.rem(i // CORES, 2) == 0, toward, half_ring)
-        return tile_at(i // (2 * CORES), dx, lax.rem(i, CORES))
+        dx = jnp.where(lax.rem(i // CORES, 2) == 0, half_ring, toward)
+        return tile_at(lax.rem(i // (2 * CORES) + tz // 2, tz), dx, lax.rem(i, CORES))
 
     def lanes(c):
         return pl.ds(c * LANES, LANES)
@@ -232,7 +232,9 @@
             a2a_copy(c, free_peer(i)).start()
             return carry
 
-        lax.fori_loop(1, nt // 2, send, 0)
+        own = tz // 2 * 2 * CORES
+        lax.fori_loop(0, own, send, 0)
+        lax.fori_loop(own + 1, nt // 2, send, 0)
 
     def send_shared(c):
         def send(i, carry):
@@ -251,6 +253,21 @@
 
     for c in range(chunks):
         own_planes(c).start()
+
+    def pass_on(n, h):
+        @pl.when(has_outer)
+        def _():
+            if n == 0:
+                for c in range(h * chunks // 2, (h + 1) * chunks // 2):
+                    outer_copy(c).wait_recv()
+            for d in range(2):
+                if n > 0:
+                    pass_copy(n - 1, h, d).wait_recv()
+                if n < 2:
+                    pass_copy(n, h, d).start()
+
+    pass_on(0, 0)
+    pass_on(0, 1)
 
     def total(ref, count):
         return lax.fori_loop(1, count, lambda a, s: s + ref[0, a], ref[0, 0])
@@ -351,20 +368,6 @@
 
         return body
 
-    def pass_on(n, h):
-        @pl.when(has_outer)
-        def _():
-            if n == 0:
-                for c in range(h * chunks // 2, (h + 1) * chunks // 2):
-                    outer_copy(c).wait_recv()
-            for d in range(2):
-                if n > 0:
-                    pass_copy(n - 1, h, d).wait_recv()
-                if n < 2:
-                    pass_copy(n, h, d).start()
-
-    pass_on(0, 0)
-    pass_on(0, 1)
 
     @pl.when(jnp.logical_not(has_outer))
     def _():
@@ -377,29 +380,39 @@
 
     for c in range(chunks):
         load_est(c).wait()
-    lax.fori_loop(half_y, half_y + ny, blur_z(0), 0)
-    pass_on(1, 0)
-    lax.fori_loop(half_y, half_y + ny, blur_z(1), 0)
+    def blur_own(h):
+        lax.fori_loop(half_y, half_y + ny, blur_z(h), 0)
+        if h == 0:
+            pass_on(1, h)
+        lax.fori_loop(pad, ny - pad, blur_y(h), 0)
+
+    blur_own(0)
+    lax.fori_loop(pad // ygroup, (ny - pad) // ygroup, blur_x((0,)), 0)
     pass_on(1, 1)
-    for h in range(2):
-        lax.fori_loop(pad, ny - pad, blur_y(h), 0)
-    lax.fori_loop(pad // ygroup, (ny - pad) // ygroup, blur_x(range(chunks)), 0)
-
-    def blur_edges(h):
-        for c in range(h * chunks // 2, (h + 1) * chunks // 2):
-            inner_copy(c).wait_recv()
-        pass_on(2, h)
-        for first, last in ((0, half_y), (half_y + ny, ny + 2 * half_y)):
-            lax.fori_loop(first, last, blur_z(h), 0)
-        for first, last in ((0, pad), (ny - pad, ny)):
-            lax.fori_loop(first, last, blur_y(h), 0)
-
-    def blur_x_rest(cs):
-        for first, last in ((0, pad), (ny - pad, ny)):
-            lax.fori_loop(first // ygroup, last // ygroup, blur_x(cs), 0)
-
-    blur_edges(0)
-    blur_x_rest((0,))
+
+    def side_start(inner, last):
+        return jnp.where((core == 0) == inner, last, 0)
+
+    def from_row(body, first):
+        return lambda i, carry: body(first + i, carry)
+
+    def blur_edge(h, inner):
+        if inner:
+            for c in range(h * chunks // 2, (h + 1) * chunks // 2):
+                inner_copy(c).wait_recv()
+        else:
+            pass_on(2, h)
+        lax.fori_loop(0, half_y, from_row(blur_z(h), side_start(inner, half_y + ny)), 0)
+        lax.fori_loop(0, pad, from_row(blur_y(h), side_start(inner, ny - pad)), 0)
+
+    def blur_x_edge(cs, inner):
+        first = side_start(inner, (ny - pad) // ygroup)
+        lax.fori_loop(0, pad // ygroup, from_row(blur_x(cs), first), 0)
+
+    blur_edge(0, True)
+    blur_x_edge((0,), True)
+    blur_edge(0, False)
+    blur_x_edge((0,), False)
 
     halo = jnp.zeros((half_y, nz, nx), F32)
 
@@ -453,7 +466,16 @@
         def _():
             qh_copy(c, 1).start()
 
-    def back_pairs(c, first, last):
+    def back_rows(c, first, count):
+        def body(i, carry):
+            r = x_pass(wxt, zb, i * ygroup, ygroup, c, 0).reshape(ygroup, nz, LANES)
+            for k in range(ygroup):
+                reg_rows[c, pl.ds(i * ygroup + k, nz, stride=ny), :] = cov * r[k]
+            return carry
+
+        lax.fori_loop(0, count // ygroup, from_row(body, first // ygroup), 0)
+
+    def back_pairs(c, first, count):
         def body(i, carry):
             for k in range(2):
                 acc = py_ref[0, ky - 1] * q_ext[2 * i + k, :, lanes(c)]
@@ -465,22 +487,36 @@
                 zb[2 * i + k, :, lanes(c)] = r[:, k * LANES : (k + 1) * LANES]
             return carry
 
-        lax.fori_loop(first // 2, last // 2, body, 0)
+        lax.fori_loop(0, count // 2, from_row(body, first // 2), 0)
 
     def back_inner(c):
-        back_pairs(c, pad, ny - pad)
-
-    def back_outer(c):
-        @pl.when(has_left)
+        back_pairs(c, pad, ny - 2 * pad)
+
+        @pl.when(core == 0)
+        def _():
+            qh_copy(c, 0).wait_recv()
+
+        @pl.when(core == 1)
         def _():
             qh_copy(c, 1).wait_recv()
 
-        @pl.when(has_right)
+        first = side_start(True, ny - pad)
+        back_pairs(c, first, pad)
+        back_rows(c, pad, ny - 2 * pad)
+        back_rows(c, first, pad)
+
+    def back_outer(c):
+        @pl.when(jnp.logical_and(core == 0, has_left))
+        def _():
+            qh_copy(c, 1).wait_recv()
+
+        @pl.when(jnp.logical_and(core == 1, has_right))
         def _():
             qh_copy(c, 0).wait_recv()
 
-        back_pairs(c, 0, pad)
-        back_pairs(c, ny - pad, ny)
+        first = side_start(False, ny - pad)
+        back_pairs(c, first, pad)
+        back_rows(c, first, pad)
 
     sums = reg
     strip_rows = strip.reshape(strip_planes * ny, LANES)
@@ -495,15 +531,6 @@
                 v = jnp.where(in_strip, cov * r[k], 0.0)
                 v = jnp.sum(v.reshape(strip_planes, packed, LANES), axis=1)
                 strip_rows[pl.ds(i * ygroup + k, strip_planes, stride=ny), :] = v
-            return carry
-
-        lax.fori_loop(0, ny // ygroup, body, 0)
-
-    def back_x(c):
-        def body(i, carry):
-            r = x_pass(wxt, zb, i * ygroup, ygroup, c, 0).reshape(ygroup, nz, LANES)
-            for k in range(ygroup):
-                reg_rows[c, pl.ds(i * ygroup + k, nz, stride=ny), :] = cov * r[k]
             return carry
 
         lax.fori_loop(0, ny // ygroup, body, 0)
@@ -646,48 +673,46 @@
 
     quotient(0)
     send_shared(1)
-    send_free(2)
     back_inner(0)
-    blur_edges(1)
+    blur_own(1)
+    blur_edge(1, True)
     back_outer(0)
-    back_x(0)
     stage1(0)
-    blur_x_rest((1,))
+    blur_edge(1, False)
+    lax.fori_loop(0, ny // ygroup, blur_x((1,)), 0)
     stage2(0)
     quotient(1)
     send_shared(2)
-    send_free(3)
+    send_free(2)
     back_inner(1)
     stage3(0)
     back_outer(1)
-    back_x(1)
     stage1(1)
-    blur_x_rest((2, 3))
+    lax.fori_loop(0, ny // ygroup, blur_x((2, 3)), 0)
     stage4(0)
     stage2(1)
     quotient(2)
     send_shared(3)
+    send_free(3)
     back_inner(2)
     stage3(1)
     back_outer(2)
-    back_x(2)
     stage1(2)
     stage5(0)
     stage4(1)
+    quotient(3)
     stage2(2)
-    quotient(3)
     back_inner(3)
+    back_outer(3)
+    stage1(3)
     stage3(2)
-    back_outer(3)
-    back_x(3)
-    stage1(3)
     back_strip()
     stage1(chunks)
     stage5(1)
     realign(0)
-    stage4(2)
     stage2(3)
     stage2(chunks)
+    stage4(2)
     stage3(3)
     stage3(chunks)
     stage5(2)

time: 181 us -> 175 us (0.967)
  Pallas kernels: 178 us -> 171 us
    pallas_call x1, Pallas kernels: 178 us -> 171 us  [on_device(): pl.pallas_call(functools.partial(rl_kernel, dims), out_shape=pltpu.VMEM(e...]
where the time goes in v5:
time: 175 us; the launch traced here: 174 us
  Pallas kernels  171 us (98%)
  local copies, waits for them, and re-layouts  2.71 us (2%)
    pallas_call x1, Pallas kernels, on_device(): pl.pallas_call(functools.partial(rl_kernel, dims), out_shape=pltpu.VMEM(e...  171 us

profile of v5, /device:TPU:32, one launch (start us, length us, event | category | flops | bytes accessed | tf_op | source)
XLA Modules:
  0.0 174.5 jit_solution(8342192801766515815)
XLA Ops:
  0.7 171.1 %shard_map.73 = f32[128,24,512]{2,1,0:T(8,128)S(1)} custom-call(f32[128,24,512]{2,1,0:T(8,128)} %est_hbm.1, f32[1,4,768,512]{3,2,1,0:T(8,128)} %stack_hbm.1, f32[1,31]{1,0:T(1,128)} %pz_ref.1, f32[1,15]{1,0:T(1,128)} %py_ref.1, f32[1,15]{1,0:T(1,128)} %px_ref.1, s32[1]{0:T(128)S(6)} %copy.10.off_ref, s32[1,4]{1,0:T(1,128)} %cov_ref.1), custom_call_target="tpu_custom_call" | custom-call | tf_op jit(solution)/shard_map/pallas_call | solution.py:779
  171.8 2.7 %copy.9 = f32[128,24,512]{2,1,0:T(8,128)} copy(f32[128,24,512]{2,1,0:T(8,128)S(1)} %shard_map.73) | data formatting | bytes 12582912

commit v6 on v5

--- a/solution.py
+++ b/solution.py
@@ -456,15 +456,27 @@
             q_ext[half_y + y, :, lanes(c)] = v / q_ext[half_y + y, :, lanes(c)]
             return carry
 
-        lax.fori_loop(0, ny, body, 0)
-
-        @pl.when(has_left)
+        lax.fori_loop(0, pad, from_row(body, side_start(False, ny - pad)), 0)
+
+        @pl.when(jnp.logical_and(core == 0, has_left))
         def _():
             qh_copy(c, 0).start()
 
-        @pl.when(has_right)
+        @pl.when(jnp.logical_and(core == 1, has_right))
         def _():
             qh_copy(c, 1).start()
+
+        lax.fori_loop(0, pad, from_row(body, side_start(True, ny - pad)), 0)
+
+        @pl.when(core == 0)
+        def _():
+            qh_copy(c, 1).start()
+
+        @pl.when(core == 1)
+        def _():
+            qh_copy(c, 0).start()
+
+        lax.fori_loop(pad, ny - pad, body, 0)
 
     def back_rows(c, first, count):
         def body(i, carry):

time: 175 us -> 174 us (level)
  no operation moved by 1% of the time
where the time goes in v6:
time: 174 us
  Pallas kernels  170 us (98%)
  local copies, waits for them, and re-layouts  2.71 us (2%)
    pallas_call x1, Pallas kernels, on_device(): pl.pallas_call(functools.partial(rl_kernel, dims), out_shape=pltpu.VMEM(e...  170 us

profile of v6, /device:TPU:32, one launch (start us, length us, event | category | flops | bytes accessed | tf_op | source)
XLA Modules:
  0.0 173.8 jit_solution(3611900506233164014)
XLA Ops:
  0.7 170.4 %shard_map.73 = f32[128,24,512]{2,1,0:T(8,128)S(1)} custom-call(f32[128,24,512]{2,1,0:T(8,128)} %est_hbm.1, f32[1,4,768,512]{3,2,1,0:T(8,128)} %stack_hbm.1, f32[1,31]{1,0:T(1,128)} %pz_ref.1, f32[1,15]{1,0:T(1,128)} %py_ref.1, f32[1,15]{1,0:T(1,128)} %px_ref.1, s32[1]{0:T(128)S(6)} %copy.10.off_ref, s32[1,4]{1,0:T(1,128)} %cov_ref.1), custom_call_target="tpu_custom_call" | custom-call | tf_op jit(solution)/shard_map/pallas_call | solution.py:791
  171.1 2.7 %copy.9 = f32[128,24,512]{2,1,0:T(8,128)} copy(f32[128,24,512]{2,1,0:T(8,128)S(1)} %shard_map.73) | data formatting | bytes 12582912
